TPU v7x, 128 devices: a whole 4x4x4 slice. The times are simulated.
128 devices in a mesh: grp: 8 (over y, core), blk: 16 (over z, x).
Axes of the slice: x: 4, y: 4, z: 4, core: 2. Of those that a mesh axis runs over, the one named last changes fastest.
Arguments:
- void_fraction: float32 [256, 128, 2048], P('blk', None, 'grp'), parts along dimension 2, may hold values from 0.5 to 0.95
- slip_velocity: float32 [3, 256, 128, 2048], P(None, 'blk', None, 'grp'), parts along dimension 3, may hold values from -10.5 to 10.5
- size_class: int32 [32, 16, 256], P('blk', None, 'grp'), parts along dimension 2, may hold values from 0 to 3
- class_scale: float32 [4], replicated, may hold values from 0.5 to 2
Outputs:
- corrected_drag: float32 [3, 256, 128, 2048], P(None, 'blk', None, 'grp'), parts along dimension 3
There are 8 independent parts, one for each index of `grp`. A program takes and returns all parts, laid end to end along the dimension named above; an argument that names none is the same for every part. Nothing has to cross between parts.
All inputs are finite; a program needn't handle non-finite values.
Results may differ from a plain program's by a relative error of at most 0.00025.
Values sent between devices are 32-bit elements; how exact they have to be, the bound alone decides.
No kernel may reach another device: no remote copies, remote signals or barrier semaphores. Data moves between devices by JAX's collectives and lax.ppermute only.
A program may use at most 128 MiB of HBM per device.

v0:
```python
import jax
import jax.numpy as jnp
from jax import lax
from jax.sharding import PartitionSpec as P


def with_halo(block, sides, width):
    for axis, dim in sides:
        count = lax.axis_size(axis)
        forward = [(i, i + 1) for i in range(count - 1)]
        forward.append((count - 1, 0))
        backward = [(target, source) for source, target in forward]
        low = lax.ppermute(
            lax.slice_in_dim(block, block.shape[dim] - width, None, axis=dim), axis, forward
        )
        high = lax.ppermute(lax.slice_in_dim(block, 0, width, axis=dim), axis, backward)
        block = jnp.concatenate([low, block, high], axis=dim)
    return block


def restrict_table(length, periodic):
    fine = jnp.arange(length, dtype=jnp.int32)[:, None]
    coarse = jnp.arange(length // 2, dtype=jnp.int32)[None, :]
    table = jnp.zeros((length, length // 2), jnp.float32)
    for offset, weight in ((-1, 0.125), (0, 0.375), (1, 0.375), (2, 0.125)):
        source = 2 * coarse + offset
        if periodic:
            source = source % length
        else:
            source = jnp.clip(source, 0, length - 1)
        table = table + jnp.where(source == fine, weight, 0.0)
    return table


def prolong_table(length, periodic):
    coarse = jnp.arange(length, dtype=jnp.int32)[:, None]
    fine = jnp.arange(2 * length, dtype=jnp.int32)[None, :]
    centre = fine // 2
    neighbour = centre - 1 + 2 * (fine % 2)
    if periodic:
        neighbour = neighbour % length
    else:
        neighbour = jnp.clip(neighbour, 0, length - 1)
    return jnp.where(coarse == centre, 0.75, 0.0) + jnp.where(coarse == neighbour, 0.25, 0.0)


def along_last(values, table):
    return jnp.dot(values, table, precision=lax.Precision.HIGHEST)


def along_second(values, table):
    return jnp.einsum("cxyz,yw->cxwz", values, table, precision=lax.Precision.HIGHEST)


def restrict_minor(values):
    halved = along_second(values, restrict_table(values.shape[2], True))
    return along_last(halved, restrict_table(values.shape[3], False))


def prolong_minor(values):
    doubled = along_second(values, prolong_table(values.shape[2], True))
    return along_last(doubled, prolong_table(values.shape[3], False))


def restrict_first(padded):
    inner_rows = padded.shape[1] - 2
    first_cells = padded[:, 0:inner_rows:2]
    second_cells = padded[:, 1 : inner_rows + 1 : 2]
    third_cells = padded[:, 2 : inner_rows + 2 : 2]
    fourth_cells = padded[:, 3 : inner_rows + 2 : 2]
    return (first_cells + 3.0 * second_cells + 3.0 * third_cells + fourth_cells) * 0.125


def prolong_first(padded):
    inner_rows = padded.shape[1] - 2
    centre = padded[:, 1 : inner_rows + 1]
    behind = padded[:, 0:inner_rows]
    ahead_cells = padded[:, 2 : inner_rows + 2]
    lower_cells = (3.0 * centre + behind) * 0.25
    upper_cells = (3.0 * centre + ahead_cells) * 0.25
    new_shape = list(centre.shape)
    new_shape[1] = 2 * inner_rows
    return jnp.stack([lower_cells, upper_cells], 2).reshape(new_shape)


def restrict_padded(padded):
    return restrict_minor(restrict_first(padded))


def prolong_padded(padded):
    return prolong_minor(prolong_first(padded))


def drag_force(void_level, slip_level, kappa_field):
    slip_speed = jnp.sqrt(jnp.sum(slip_level * slip_level, axis=0))
    factor = kappa_field * (1.0 - void_level) * jnp.exp(-1.65 * jnp.log(void_level)) * slip_speed
    return factor[None] * slip_level


def class_lookup(size_class, class_scale):
    labels = jnp.arange(class_scale.shape[0], dtype=jnp.int32)
    chosen = jnp.where(size_class[..., None] == labels, class_scale, 0.0)
    return jnp.sum(chosen, axis=-1)


def expand_blocks(block_values, repeat_count):
    extent_x, extent_y, extent_z = block_values.shape
    widened = jnp.broadcast_to(
        block_values[:, None, :, None, :, None],
        (extent_x, repeat_count, extent_y, repeat_count, extent_z, repeat_count),
    )
    return widened.reshape(
        extent_x * repeat_count, extent_y * repeat_count, extent_z * repeat_count
    )


def plane_terms(filtered, slip_level, drag_level):
    return (
        jnp.sum(filtered * slip_level, axis=(0, 1, 2)),
        jnp.sum(drag_level * slip_level, axis=(0, 1, 2)),
    )


def level_sum(terms):
    return lax.psum((terms[0], terms[1]), "blk")


def spread_rim(values):
    padded = with_halo(values, (("blk", 1),), 1)
    return prolong_padded(padded)


def shards(void_fraction, slip_velocity, size_class, class_scale):
    kappa_block = class_lookup(size_class, class_scale)
    void_level = void_fraction
    slip_level = slip_velocity
    drag_levels = []
    filtered_levels = []
    slip_levels = []
    for level_index in range(2):
        kappa_level = expand_blocks(kappa_block, 8 >> level_index)
        drag_level = drag_force(void_level, slip_level, kappa_level)
        stacked = jnp.concatenate([void_level[None], slip_level, drag_level], 0)
        padded = with_halo(stacked, (("blk", 1),), 1)
        coarse = restrict_padded(padded)
        drag_levels.append(drag_level)
        void_level = coarse[0]
        slip_level = coarse[1:4]
        filtered_levels.append(coarse[4:7])
        slip_levels.append(slip_level)
    drag_two = drag_force(void_level, slip_level, expand_blocks(kappa_block, 2))
    first_terms = plane_terms(filtered_levels[0], slip_levels[0], drag_levels[1])
    second_terms = plane_terms(filtered_levels[1], slip_levels[1], drag_two)
    numerator_one, denominator_one = level_sum(first_terms)
    numerator_two, denominator_two = level_sum(second_terms)
    stacked_two = jnp.concatenate([void_level[None], slip_level, drag_two], 0)
    padded_two = with_halo(stacked_two, (("blk", 1),), 1)
    coarse_three = restrict_padded(padded_two)
    drag_three = drag_force(coarse_three[0], coarse_three[1:4], kappa_block)
    terms_three = plane_terms(coarse_three[4:7], coarse_three[1:4], drag_three)
    numerator_three, denominator_three = lax.psum((terms_three[0], terms_three[1]), "blk")
    correction_three = (numerator_three / denominator_three - 1.0) * drag_three
    padded_three = with_halo(correction_three, (("blk", 1),), 1)
    correction = prolong_padded(padded_three)
    correction = correction + (numerator_two / denominator_two - 1.0) * drag_two
    correction = spread_rim(correction) + (numerator_one / denominator_one - 1.0) * drag_levels[1]
    return drag_levels[0] + spread_rim(correction)


def solution(mesh):
    return jax.shard_map(
        shards,
        mesh=mesh,
        in_specs=(P("blk", None, "grp"), P(None, "blk", None, "grp"), P("blk", None, "grp"), P()),
        out_specs=P(None, "blk", None, "grp"),
        check_vma=False,
    )
```

profile of v0, /device:TPU:0, one launch (start us, length us, event | category | flops | bytes accessed | tf_op | source)
XLA Modules:
  0.0 205.8 jit_solution(10027364828599188503)
XLA Ops:
  0.8 11.4 %broadcast_in_dim.200 = f32[2,8,16,8,32,8]{5,4,3,2,1,0:T(8,128)} broadcast(f32[2,16,32]{2,1,0:T(8,128)S(1)} %select_reduce_fusion), dimensions={0,2,4} | broadcast | bytes 2101248 | tf_op jit(solution)/shard_map/broadcast_in_dim | solution.py:108
  12.2 25.2 %reshape.634 = f32[16,128,256]{2,1,0:T(8,128)} reshape(f32[2,8,16,8,32,8]{5,4,3,2,1,0:T(8,128)} %broadcast_in_dim.200) | data formatting | bytes 4194304 | tf_op jit(solution)/shard_map/reshape | solution.py:112
  37.4 3.9 %multiply_reduce_fusion = f32[16,128,256]{2,1,0:T(8,128)S(1)} fusion(f32[3,16,128,256]{3,2,1,0:T(8,128)} %param.5), kind=kLoop, calls=%fused_computation.13 | loop fusion | flops 2621440 | bytes 8388608 | tf_op jit(solution)/shard_map/reduce_sum | solution.py:95
  41.5 1.1 sqrt_multiply_fusion
  43.5 0.9 broadcast_multiply_fusion
  44.4 6.2 %pad_maximum_fusion.1 = f32[7,16,128,256]{3,2,1,0:T(8,128)} fusion(f32[3,16,128,256]{3,2,1,0:T(8,128)S(1)} %broadcast_multiply_fusion, f32[3,16,128,256]{3,2,1,0:T(8,128)S(1)} %bitcast.132, f32[1,16,128,256]{3,2,1,0:T(8,128)S(1)} %bitcast.135), kind=kLoop, calls=%fused_computation.1 | loop fusion | flops 7340032 | bytes 29360128 | tf_op jit(solution)/shard_map/concatenate | solution.py:143
  50.6 0.9 copy-done
  51.5 2.9 %fusion.297 = (f32[7,1,128,256]{3,2,1,0:T(8,128)}, f32[7,1,128,256]{3,2,1,0:T(8,128)}) fusion(f32[7,16,128,256]{3,2,1,0:T(8,128)} %pad_maximum_fusion.1), kind=kLoop, calls=%fused_computation.456 | loop fusion | bytes 3670016 | tf_op jit(solution)/shard_map/slice | solution.py:14
  54.4 1.6 collective-permute-start
  56.0 4.7 %collective-permute-start.1 = (f32[7,1,128,256]{3,2,1,0:T(8,128)}, f32[7,1,128,256]{3,2,1,0:T(8,128)}, u32[]{:S(2)}, u32[]{:S(2)}) collective-permute-start(f32[7,1,128,256]{3,2,1,0:T(8,128)} %get-tuple-element.20), channel_id=1, source_target_pairs={{1,0},{2,1},{3,2},{4,3},{5,4},{6,5},{7,6},{8,7},{9,8},{10,9},{11,1... | collective-permute-start | bytes 2752520 | tf_op jit(solution)/shard_map/ppermute | solution.py:16
  60.9 4.4 %broadcast_in_dim.223 = f32[2,4,16,4,32,4]{5,4,3,2,1,0:T(8,128)} broadcast(f32[2,16,32]{2,1,0:T(8,128)S(1)} %select_reduce_fusion), dimensions={0,2,4} | broadcast | bytes 266240 | tf_op jit(solution)/shard_map/broadcast_in_dim | solution.py:108
  65.3 8.2 %reshape.635 = f32[1,8,64,128]{3,2,1,0:T(8,128)S(1)} reshape(f32[2,4,16,4,32,4]{5,4,3,2,1,0:T(8,128)} %broadcast_in_dim.223) | data formatting | bytes 524288 | tf_op jit(solution)/shard_map/reshape | solution.py:112
  73.4 1.7 broadcast_in_dim.224
  75.1 3.2 %reshape.636 = f32[1,4,32,64]{3,2,1,0:T(8,128)S(1)} reshape(f32[2,2,16,2,32,2]{5,4,3,2,1,0:T(8,128)} %broadcast_in_dim.224) | data formatting | bytes 65536 | tf_op jit(solution)/shard_map/reshape | solution.py:112
  78.5 3.0 %collective-permute-done = f32[7,1,128,256]{3,2,1,0:T(8,128)} collective-permute-done((f32[7,1,128,256]{3,2,1,0:T(8,128)}, f32[7,1,128,256]{3,2,1,0:T(8,128)}, u32[]{:S(2)}, u32[]{:S(2)}) %collective-permute-start) | collective-permute-done | bytes 917536 | tf_op jit(solution)/shard_map/ppermute | solution.py:13
  81.4 12.1 %pad_maximum_fusion = f32[7,18,128,256]{3,2,1,0:T(8,128)} fusion(f32[7,1,128,256]{3,2,1,0:T(8,128)} %collective-permute-done.1, f32[3,16,128,256]{3,2,1,0:T(8,128)} %copy-done, f32[3,16,128,256]{3,2,1,0:T(8,128)} %param.5, f32[1,16,128,256]{3,2,1,0:T(8,128)S(1)} %bitcast.136, f32[7,1,128,256]{3,2,1,0:T(8,128)} %collective-permute-done), kind=kLoop, calls=%fused_computation | loop fusion | flops 16515072 | bytes 33030144 | tf_op jit(solution)/shard_map/concatenate | solution.py:17
  93.6 10.5 %fusion = f32[64,7,8,256]{3,0,2,1:T(8,128)S(1)} fusion(f32[7,18,128,256]{3,2,1,0:T(8,128)} %pad_maximum_fusion, f32[7,16,128,256]{3,2,1,0:T(8,128)S(1)} %bitcast.134, s32[64]{0:T(128)S(1)} %get-tuple-element.37, s32[64]{0:T(128)S(1)} %get-tuple-element.38, s32[64]{0:T(128)S(1)} %get-tuple-element.39, s32[64]{0:T(128)S(1)} %get-tuple-element.40), kind=kOutput, calls=%fused_computation.2 | convolution fusion | flops 1420386304 | bytes 33032192 | tf_op jit(solution)/shard_map/cxyz,yw->cxwz/dot_general | solution.py:52
  104.1 3.1 %fusion.11 = f32[7,8,64,128]{3,2,1,0:T(8,128)S(1)} fusion(f32[64,7,8,256]{3,0,2,1:T(8,128)S(1)} %fusion, s32[128]{0:T(128)S(1)} %get-tuple-element.41, s32[128]{0:T(128)S(1)} %get-tuple-element.42, s32[128]{0:T(128)S(1)} %get-tuple-element.44, s32[128]{0:T(128)S(1)} %get-tuple-element.43), kind=kOutput, calls=%fused_computation.14 | convolution fusion | flops 1409646592 | bytes 5507072 | tf_op jit(solution)/shard_map/dot_general | solution.py:48
  108.0 5.3 %collective-permute-start.3 = (f32[7,1,64,128]{3,2,1,0:T(8,128)S(1)}, f32[7,1,64,128]{3,2,1,0:T(8,128)S(1)}, u32[]{:S(2)}, u32[]{:S(2)}) collective-permute-start(f32[7,1,64,128]{3,2,1,0:T(8,128)S(1)} %get-tuple-element.22), channel_id=1, source_target_pairs={{1,0},{2,1},{3,2},{4,3},{5,4},{6,5},{7,6},{8,7},{9,8},{10,9},{11,1... | collective-permute-start | bytes 688136 | tf_op jit(solution)/shard_map/ppermute | solution.py:16
  113.5 5.1 %collective-permute-done.2 = f32[7,1,64,128]{3,2,1,0:T(8,128)S(1)} collective-permute-done((f32[7,1,64,128]{3,2,1,0:T(8,128)S(1)}, f32[7,1,64,128]{3,2,1,0:T(8,128)S(1)}, u32[]{:S(2)}, u32[]{:S(2)}) %collective-permute-start.2) | collective-permute-done | bytes 229408 | tf_op jit(solution)/shard_map/ppermute | solution.py:13
  120.5 5.3 %collective-permute-start.5 = (f32[7,1,32,64]{3,2,1,0:T(8,128)S(1)}, f32[7,1,32,64]{3,2,1,0:T(8,128)S(1)}, u32[]{:S(2)}, u32[]{:S(2)}) collective-permute-start(f32[7,1,32,64]{3,2,1,0:T(8,128)S(1)} %get-tuple-element.28), channel_id=1, source_target_pairs={{1,0},{2,1},{3,2},{4,3},{5,4},{6,5},{7,6},{8,7},{9,8},{10,9},{11,1... | collective-permute-start | bytes 172040 | tf_op jit(solution)/shard_map/ppermute | solution.py:16
  125.9 2.7 %collective-permute-done.4 = f32[7,1,32,64]{3,2,1,0:T(8,128)S(1)} collective-permute-done((f32[7,1,32,64]{3,2,1,0:T(8,128)S(1)}, f32[7,1,32,64]{3,2,1,0:T(8,128)S(1)}, u32[]{:S(2)}, u32[]{:S(2)}) %collective-permute-start.4) | collective-permute-done | bytes 57376 | tf_op jit(solution)/shard_map/ppermute | solution.py:13
  129.4 40.8 %all-reduce = (f32[32]{0:T(128)S(1)}, f32[32]{0:T(128)S(1)}, f32[64]{0:T(128)S(1)}, f32[64]{0:T(128)S(1)}, f32[128]{0:T(128)S(1)}, /*index=5*/f32[128]{0:T(128)S(1)}) all-reduce(f32[32]{0:T(128)S(1)} %get-tuple-element.10, f32[32]{0:T(128)S(1)} %get-tuple-element.9, ...), channel_id=1, replica_groups=mesh['grp'=8,'blk'=16] {'blk'}, use_global_device_ids=true, to_apply=%region_5.6 | all-reduce | flops 448 | bytes 3584 | tf_op jit(solution)/shard_map/psum | solution.py:161
  170.3 5.3 %collective-permute-start.7 = (f32[3,1,16,32]{3,2,1,0:T(8,128)S(1)}, f32[3,1,16,32]{3,2,1,0:T(8,128)S(1)}, u32[]{:S(2)}, u32[]{:S(2)}) collective-permute-start(f32[3,1,16,32]{3,2,1,0:T(8,128)S(1)} %get-tuple-element.36), channel_id=1, source_target_pairs={{1,0},{2,1},{3,2},{4,3},{5,4},{6,5},{7,6},{8,7},{9,8},{10,9},{11,1... | collective-permute-start | bytes 18440 | tf_op jit(solution)/shard_map/ppermute | solution.py:16
  175.7 1.8 collective-permute-done.6
  178.3 5.4 %collective-permute-start.9 = (f32[3,1,32,64]{3,2,1,0:T(8,128)S(1)}, f32[3,1,32,64]{3,2,1,0:T(8,128)S(1)}, u32[]{:S(2)}, u32[]{:S(2)}) collective-permute-start(f32[3,1,32,64]{3,2,1,0:T(8,128)S(1)} %get-tuple-element.32), channel_id=1, source_target_pairs={{1,0},{2,1},{3,2},{4,3},{5,4},{6,5},{7,6},{8,7},{9,8},{10,9},{11,1... | collective-permute-start | bytes 73736 | tf_op jit(solution)/shard_map/ppermute | solution.py:16
  183.7 2.0 collective-permute-done.8
  185.8 0.8 convolution_bitcast_fusion
  187.6 5.8 %collective-permute-start.11 = (f32[3,1,64,128]{3,2,1,0:T(8,128)S(1)}, f32[3,1,64,128]{3,2,1,0:T(8,128)S(1)}, u32[]{:S(2)}, u32[]{:S(2)}) collective-permute-start(f32[3,1,64,128]{3,2,1,0:T(8,128)S(1)} %get-tuple-element.26), channel_id=1, source_target_pairs={{1,0},{2,1},{3,2},{4,3},{5,4},{6,5},{7,6},{8,7},{9,8},{10,9},{11,1... | collective-permute-start | bytes 294920 | tf_op jit(solution)/shard_map/ppermute | solution.py:16
  193.3 2.2 %collective-permute-done.10 = f32[3,1,64,128]{3,2,1,0:T(8,128)S(1)} collective-permute-done((f32[3,1,64,128]{3,2,1,0:T(8,128)S(1)}, f32[3,1,64,128]{3,2,1,0:T(8,128)S(1)}, u32[]{:S(2)}, u32[]{:S(2)}) %collective-permute-start.10) | collective-permute-done | bytes 98336 | tf_op jit(solution)/shard_map/ppermute | solution.py:13
  196.2 2.7 %fusion.97 = f32[128,3,16,128]{3,0,2,1:T(8,128)S(1)} fusion(f32[3,16,64,128]{3,2,1,0:T(8,128)S(1)} %bitcast.137, s32[128]{0:T(128)S(1)} %and_select_fusion.20, s32[128]{0:T(128)S(1)} %get-tuple-element.65), kind=kOutput, calls=%fused_computation.169 | convolution fusion | flops 604020736 | bytes 4719616 | tf_op jit(solution)/shard_map/cxyz,yw->cxwz/dot_general | solution.py:52
  198.9 6.9 %fusion.17 = f32[3,16,128,256]{3,2,1,0:T(8,128)} fusion(f32[3,16,128,256]{3,2,1,0:T(8,128)S(1)} %bitcast.130, f32[128,3,16,128]{3,0,2,1:T(8,128)S(1)} %fusion.97, s32[256]{0:T(256)S(1)} %get-tuple-element.68, s32[256]{0:T(256)S(1)} %get-tuple-element.67), kind=kOutput, calls=%fused_computation.21 | convolution fusion | flops 2417655808 | bytes 15730688 | tf_op jit(solution)/shard_map/dot_general | solution.py:48
  (94 shorter events, 8.1 us)
Async XLA Ops:
  37.4 4.0 %copy-start.1 = (f32[16,128,256]{2,1,0:T(8,128)S(1)}, f32[16,128,256]{2,1,0:T(8,128)}, u32[]{:S(2)}) copy-start(f32[16,128,256]{2,1,0:T(8,128)} %param.4) | copy-start | bytes 6291460
  37.4 4.0 %copy-start.2 = (f32[16,128,256]{2,1,0:T(8,128)S(1)}, f32[16,128,256]{2,1,0:T(8,128)}, u32[]{:S(2)}) copy-start(f32[16,128,256]{2,1,0:T(8,128)} %reshape.634) | copy-start | bytes 6291460
  37.4 5.3 %slice-start.2 = ((s8[6291456]{0:T(1024)(128)(4,1)}), s8[4194304]{0:T(1024)(128)(4,1)S(1)}, s32[]{:S(2)}) async-start(s8[6291456]{0:T(1024)(128)(4,1)} %bitcast.131), calls=%async_computation.2 | async-start | bytes 8388608
  41.5 2.1 %slice-start.3 = ((s8[6291456]{0:T(1024)(128)(4,1)}), s8[2097152]{0:T(1024)(128)(4,1)S(1)}, s32[]{:S(2)}) async-start(s8[6291456]{0:T(1024)(128)(4,1)} %bitcast.131), calls=%async_computation.3 | async-start | bytes 4194304
  44.4 7.1 %copy-start = (f32[3,16,128,256]{3,2,1,0:T(8,128)}, f32[3,16,128,256]{3,2,1,0:T(8,128)S(1)}, u32[]{:S(2)}) copy-start(f32[3,16,128,256]{3,2,1,0:T(8,128)S(1)} %broadcast_multiply_fusion) | copy-start | bytes 18874372
  54.4 27.0 %collective-permute-start = (f32[7,1,128,256]{3,2,1,0:T(8,128)}, f32[7,1,128,256]{3,2,1,0:T(8,128)}, u32[]{:S(2)}, u32[]{:S(2)}) collective-permute-start(f32[7,1,128,256]{3,2,1,0:T(8,128)} %get-tuple-element.19), channel_id=1, source_target_pairs={{0,1},{1,2},{2,3},{3,4},{4,5},{5,6},{6,7},{7,8},{8,9},{9,10},{10,1... | collective-permute-start | bytes 2752520 | tf_op jit(solution)/shard_map/ppermute | solution.py:13
  56.0 25.4 %collective-permute-start.1 = (f32[7,1,128,256]{3,2,1,0:T(8,128)}, f32[7,1,128,256]{3,2,1,0:T(8,128)}, u32[]{:S(2)}, u32[]{:S(2)}) collective-permute-start(f32[7,1,128,256]{3,2,1,0:T(8,128)} %get-tuple-element.20), channel_id=1, source_target_pairs={{1,0},{2,1},{3,2},{4,3},{5,4},{6,5},{7,6},{8,7},{9,8},{10,9},{11,1... | collective-permute-start | bytes 2752520 | tf_op jit(solution)/shard_map/ppermute | solution.py:16
  78.4 15.1 %slice-start.4 = ((s8[14680064]{0:T(1024)(128)(4,1)}), s8[4194304]{0:T(1024)(128)(4,1)S(1)}, s32[]{:S(2)}) async-start(s8[14680064]{0:T(1024)(128)(4,1)} %bitcast.133), calls=%async_computation.4 | async-start | bytes 8388608
  78.4 15.1 %slice-start.5 = ((s8[14680064]{0:T(1024)(128)(4,1)}), s8[4194304]{0:T(1024)(128)(4,1)S(1)}, s32[]{:S(2)}) async-start(s8[14680064]{0:T(1024)(128)(4,1)} %bitcast.133), calls=%async_computation.5 | async-start | bytes 8388608
  78.4 15.1 %slice-start.6 = ((s8[14680064]{0:T(1024)(128)(4,1)}), s8[4194304]{0:T(1024)(128)(4,1)S(1)}, s32[]{:S(2)}) async-start(s8[14680064]{0:T(1024)(128)(4,1)} %bitcast.133), calls=%async_computation.6 | async-start | bytes 8388608
  78.5 15.1 %slice-start.7 = ((s8[14680064]{0:T(1024)(128)(4,1)}), s8[2097152]{0:T(1024)(128)(4,1)S(1)}, s32[]{:S(2)}) async-start(s8[14680064]{0:T(1024)(128)(4,1)} %bitcast.133), calls=%async_computation.7 | async-start | bytes 4194304
  107.9 10.7 %collective-permute-start.2 = (f32[7,1,64,128]{3,2,1,0:T(8,128)S(1)}, f32[7,1,64,128]{3,2,1,0:T(8,128)S(1)}, u32[]{:S(2)}, u32[]{:S(2)}) collective-permute-start(f32[7,1,64,128]{3,2,1,0:T(8,128)S(1)} %get-tuple-element.21), channel_id=1, source_target_pairs={{0,1},{1,2},{2,3},{3,4},{4,5},{5,6},{6,7},{7,8},{8,9},{9,10},{10,1... | collective-permute-start | bytes 688136 | tf_op jit(solution)/shard_map/ppermute | solution.py:13
  108.0 10.6 %collective-permute-start.3 = (f32[7,1,64,128]{3,2,1,0:T(8,128)S(1)}, f32[7,1,64,128]{3,2,1,0:T(8,128)S(1)}, u32[]{:S(2)}, u32[]{:S(2)}) collective-permute-start(f32[7,1,64,128]{3,2,1,0:T(8,128)S(1)} %get-tuple-element.22), channel_id=1, source_target_pairs={{1,0},{2,1},{3,2},{4,3},{5,4},{6,5},{7,6},{8,7},{9,8},{10,9},{11,1... | collective-permute-start | bytes 688136 | tf_op jit(solution)/shard_map/ppermute | solution.py:16
  120.4 8.2 %collective-permute-start.4 = (f32[7,1,32,64]{3,2,1,0:T(8,128)S(1)}, f32[7,1,32,64]{3,2,1,0:T(8,128)S(1)}, u32[]{:S(2)}, u32[]{:S(2)}) collective-permute-start(f32[7,1,32,64]{3,2,1,0:T(8,128)S(1)} %get-tuple-element.27), channel_id=1, source_target_pairs={{0,1},{1,2},{2,3},{3,4},{4,5},{5,6},{6,7},{7,8},{8,9},{9,10},{10,1... | collective-permute-start | bytes 172040 | tf_op jit(solution)/shard_map/ppermute | solution.py:13
  120.5 8.1 %collective-permute-start.5 = (f32[7,1,32,64]{3,2,1,0:T(8,128)S(1)}, f32[7,1,32,64]{3,2,1,0:T(8,128)S(1)}, u32[]{:S(2)}, u32[]{:S(2)}) collective-permute-start(f32[7,1,32,64]{3,2,1,0:T(8,128)S(1)} %get-tuple-element.28), channel_id=1, source_target_pairs={{1,0},{2,1},{3,2},{4,3},{5,4},{6,5},{7,6},{8,7},{9,8},{10,9},{11,1... | collective-permute-start | bytes 172040 | tf_op jit(solution)/shard_map/ppermute | solution.py:16
  170.2 7.2 %collective-permute-start.6 = (f32[3,1,16,32]{3,2,1,0:T(8,128)S(1)}, f32[3,1,16,32]{3,2,1,0:T(8,128)S(1)}, u32[]{:S(2)}, u32[]{:S(2)}) collective-permute-start(f32[3,1,16,32]{3,2,1,0:T(8,128)S(1)} %get-tuple-element.35), channel_id=1, source_target_pairs={{0,1},{1,2},{2,3},{3,4},{4,5},{5,6},{6,7},{7,8},{8,9},{9,10},{10,1... | collective-permute-start | bytes 18440 | tf_op jit(solution)/shard_map/ppermute | solution.py:13
  170.3 7.1 %collective-permute-start.7 = (f32[3,1,16,32]{3,2,1,0:T(8,128)S(1)}, f32[3,1,16,32]{3,2,1,0:T(8,128)S(1)}, u32[]{:S(2)}, u32[]{:S(2)}) collective-permute-start(f32[3,1,16,32]{3,2,1,0:T(8,128)S(1)} %get-tuple-element.36), channel_id=1, source_target_pairs={{1,0},{2,1},{3,2},{4,3},{5,4},{6,5},{7,6},{8,7},{9,8},{10,9},{11,1... | collective-permute-start | bytes 18440 | tf_op jit(solution)/shard_map/ppermute | solution.py:16
  178.2 7.5 %collective-permute-start.8 = (f32[3,1,32,64]{3,2,1,0:T(8,128)S(1)}, f32[3,1,32,64]{3,2,1,0:T(8,128)S(1)}, u32[]{:S(2)}, u32[]{:S(2)}) collective-permute-start(f32[3,1,32,64]{3,2,1,0:T(8,128)S(1)} %get-tuple-element.31), channel_id=1, source_target_pairs={{0,1},{1,2},{2,3},{3,4},{4,5},{5,6},{6,7},{7,8},{8,9},{9,10},{10,1... | collective-permute-start | bytes 73736 | tf_op jit(solution)/shard_map/ppermute | solution.py:13
  178.3 7.4 %collective-permute-start.9 = (f32[3,1,32,64]{3,2,1,0:T(8,128)S(1)}, f32[3,1,32,64]{3,2,1,0:T(8,128)S(1)}, u32[]{:S(2)}, u32[]{:S(2)}) collective-permute-start(f32[3,1,32,64]{3,2,1,0:T(8,128)S(1)} %get-tuple-element.32), channel_id=1, source_target_pairs={{1,0},{2,1},{3,2},{4,3},{5,4},{6,5},{7,6},{8,7},{9,8},{10,9},{11,1... | collective-permute-start | bytes 73736 | tf_op jit(solution)/shard_map/ppermute | solution.py:16
  187.5 8.1 %collective-permute-start.10 = (f32[3,1,64,128]{3,2,1,0:T(8,128)S(1)}, f32[3,1,64,128]{3,2,1,0:T(8,128)S(1)}, u32[]{:S(2)}, u32[]{:S(2)}) collective-permute-start(f32[3,1,64,128]{3,2,1,0:T(8,128)S(1)} %get-tuple-element.25), channel_id=1, source_target_pairs={{0,1},{1,2},{2,3},{3,4},{4,5},{5,6},{6,7},{7,8},{8,9},{9,10},{10,1... | collective-permute-start | bytes 294920 | tf_op jit(solution)/shard_map/ppermute | solution.py:13
  187.6 8.0 %collective-permute-start.11 = (f32[3,1,64,128]{3,2,1,0:T(8,128)S(1)}, f32[3,1,64,128]{3,2,1,0:T(8,128)S(1)}, u32[]{:S(2)}, u32[]{:S(2)}) collective-permute-start(f32[3,1,64,128]{3,2,1,0:T(8,128)S(1)} %get-tuple-element.26), channel_id=1, source_target_pairs={{1,0},{2,1},{3,2},{4,3},{5,4},{6,5},{7,6},{8,7},{9,8},{10,9},{11,1... | collective-permute-start | bytes 294920 | tf_op jit(solution)/shard_map/ppermute | solution.py:16
  195.6 3.3 %slice-start = ((s8[6291456]{0:T(1024)(128)(4,1)}), s8[4194304]{0:T(1024)(128)(4,1)S(1)}, s32[]{:S(2)}) async-start(s8[6291456]{0:T(1024)(128)(4,1)} %bitcast.129), calls=%async_computation | async-start | bytes 8388608
  196.0 2.9 %slice-start.1 = ((s8[6291456]{0:T(1024)(128)(4,1)}), s8[2097152]{0:T(1024)(128)(4,1)S(1)}, s32[]{:S(2)}) async-start(s8[6291456]{0:T(1024)(128)(4,1)} %bitcast.129), calls=%async_computation.1 | async-start | bytes 4194304
where the time goes:
time: 207 us; the launch traced here: 206 us
  local copies, waits for them, and re-layouts  59.2 us (29%)
  blocking collectives  40.8 us (20%)
  starting transfers between devices  33.9 us (16%)
  matrix products  27.5 us (13%)
  other arithmetic  27 us (13%)
  waiting for transfers between devices  16.8 us (8%)
    psum x1, blocking collectives, shards(): lax.psum((terms_three[0], terms_three[1]), 'blk')  40.8 us
    reshape x3, local copies, waits for them, and re-layouts, expand_blocks(): widened.reshape(extent_x * repeat_count, extent_y * repeat_count, extent_...  36.6 us
    ppermute x6, starting transfers between devices, with_halo(): lax.ppermute(lax.slice_in_dim(block, 0, width, axis=dim), axis, backward)  31.9 us
    broadcast_in_dim x3, local copies, waits for them, and re-layouts, expand_blocks(): jnp.broadcast_to(block_values[:, None, :, None, :, None], (extent_x, repe...  17.5 us
    ppermute x6, waiting for transfers between devices, with_halo(): lax.ppermute(lax.slice_in_dim(block, block.shape[dim] - width, None, axis...  16.8 us
    dot_general x6, matrix products, along_second(): jnp.einsum('cxyz,yw->cxwz', values, table, precision=lax.Precision.HIGHEST)  15.5 us
    concatenate x3, other arithmetic, with_halo(): block = jnp.concatenate([low, block, high], axis=dim)  12.4 us
    dot_general x6, matrix products, along_last(): return jnp.dot(values, table, precision=lax.Precision.HIGHEST)  12.1 us
  transfers between devices with their start and end apart: 12, of which 6 were waited for; matrix products, arithmetic and copies ran while one was open for 9% of the time, Pallas kernels for 0%

commit v1 on v0

v1 whole, which is shorter than its diff:
```python
import functools

import jax
import jax.numpy as jnp
from jax import lax
from jax.experimental import pallas as pl
from jax.experimental.pallas import tpu as pltpu
from jax.sharding import PartitionSpec as P

F32 = jnp.float32
BF16 = jnp.bfloat16
ROWS = 16
NY = 128
NZ = 256
LEAD = 8


def iota(shape, axis):
    return lax.broadcasted_iota(jnp.int32, shape, axis)


def restrict_z(length, width=None, shift=0):
    width = width or length // 2
    fine = iota((length, width), 0)
    coarse = iota((length, width), 1) - shift
    offset = fine - 2 * coarse
    weight = jnp.where((offset == 0) | (offset == 1), 3.0, 0.0)
    weight = weight + jnp.where((offset == -1) | (offset == 2), 1.0, 0.0)
    weight = weight + jnp.where((fine == 0) & (coarse == 0), 1.0, 0.0)
    last = length // 2 - 1
    weight = weight + jnp.where((fine == length - 1) & (coarse == last), 1.0, 0.0)
    weight = jnp.where((coarse >= 0) & (coarse <= last), weight, 0.0)
    return (weight * (1.0 / 512.0)).astype(BF16)


def prolong_z(length):
    coarse = iota((length, 2 * length), 0)
    fine = iota((length, 2 * length), 1)
    centre = lax.shift_right_logical(fine, 1)
    neighbour = jnp.clip(centre - 1 + 2 * (fine & 1), 0, length - 1)
    weight = jnp.where(coarse == centre, 3.0, 0.0) + jnp.where(coarse == neighbour, 1.0, 0.0)
    return (weight * (1.0 / 64.0)).astype(BF16)


def spread(values, rows, lanes):
    a, b = values.shape
    along = (iota((b, lanes), 0) == iota((b, lanes), 1) // (lanes // b)).astype(BF16)
    wide = jnp.dot(values.astype(BF16), along, preferred_element_type=F32)
    if rows == a:
        return wide
    down = (iota((rows, a), 1) == iota((rows, a), 0) // (rows // a)).astype(BF16)
    return jnp.dot(down, wide.astype(BF16), preferred_element_type=F32)


def class_factor(scale_ref, classes):
    chosen = jnp.where(classes < 0.5, scale_ref[0], scale_ref[1])
    chosen = jnp.where(classes < 1.5, chosen, scale_ref[2])
    return jnp.where(classes < 2.5, chosen, scale_ref[3])


def drag(void, s0, s1, s2, kappa):
    speed = jnp.sqrt(s0 * s0 + s1 * s1 + s2 * s2)
    factor = kappa * (1.0 - void) * jnp.exp(-1.65 * jnp.log(void)) * speed
    return factor * s0, factor * s1, factor * s2


def split_store(value, hi_ref, lo_ref, start):
    hi = value.astype(BF16)
    rows = value.shape[0]
    hi_ref[pl.ds(start, rows), 0 : value.shape[1]] = hi
    lo_ref[pl.ds(start, rows), 0 : value.shape[1]] = (value - hi.astype(F32)).astype(BF16)


def dot2(hi, lo, table):
    return jnp.dot(hi, table, preferred_element_type=F32) + jnp.dot(
        lo, table, preferred_element_type=F32
    )


def wrap_rows(pad, q, rows):
    pad[q, LEAD - 1 : LEAD] = pad[q, LEAD + rows - 1 : LEAD + rows]
    pad[q, LEAD + rows : LEAD + rows + 1] = pad[q, LEAD : LEAD + 1]


def fill_pad(pad, p, part, rows, step, lanes):
    planes = -(-lanes // 128)
    for start in range(0, rows, step):
        value = part(start, step)
        rng = slice(LEAD + start, LEAD + start + step)
        if lanes < 128:
            pad[p, rng, 0:lanes] = value
        else:
            for h in range(planes):
                pad[planes * p + h, rng] = value[:, 128 * h : 128 * h + 128]
    for h in range(planes):
        wrap_rows(pad, planes * p + h, rows)


def restrict_y(pad, p, rows, hi_ref, lo_ref, out_start, lanes, step=16):
    half = rows // 2
    step = min(step, half)
    planes = -(-lanes // 128)
    width = min(lanes, 128)
    for start in range(0, half, step):
        for h in range(planes):
            at = LEAD + 2 * start
            q = planes * p + h
            outer = pad[q, pl.ds(at - 1, step, stride=2), :] + pad[q, pl.ds(at + 2, step, stride=2), :]
            inner = pad[q, pl.ds(at, step, stride=2), :] + pad[q, pl.ds(at + 1, step, stride=2), :]
            value = (outer + 3.0 * inner)[:, 0:width]
            hi = value.astype(BF16)
            rng = slice(out_start + start, out_start + start + step)
            cols = slice(128 * h, 128 * h + width)
            hi_ref[rng, cols] = hi
            lo_ref[rng, cols] = (value - hi.astype(F32)).astype(BF16)


def prolong_y(pad, p, rows, wide, q):
    step = min(rows, 32)
    for start in range(0, rows, step):
        at = LEAD + start
        centre = 3.0 * pad[p, at : at + step]
        wide[q, pl.ds(2 * start, step, stride=2), :] = centre + pad[p, at - 1 : at - 1 + step]
        wide[q, pl.ds(2 * start + 1, step, stride=2), :] = centre + pad[p, at + 1 : at + 1 + step]


def linear_kernel(void_hbm, slip_hbm, class_ref, v_ref, even_ref, odd_ref, buf, pad, hi, lo, vbuf, wbuf, pad2, pad3, sems):
    parity = lax.axis_index("blk") % 2
    pairs = ROWS // 2

    def copies(k):
        rows = pl.ds(2 * k, 2)
        return (
            pltpu.make_async_copy(void_hbm.at[rows], buf.at[0, pl.ds(2 * k + 1, 2)], sems.at[k, 0]),
            pltpu.make_async_copy(slip_hbm.at[:, rows], buf.at[pl.ds(1, 3), pl.ds(2 * k + 1, 2)], sems.at[k, 1]),
        )

    for k in range(pairs):
        for copy in copies(k):
            copy.start()
    for c in range(4):
        for row in (0, ROWS + 1):
            for start in range(0, NY, 32):
                buf[c, row, start : start + 32] = jnp.zeros((32, NZ), F32)
    table = restrict_z(NZ)
    table_lo = restrict_z(128, 128, 0)
    table_hi = restrict_z(128, 128, 64)
    table3 = [restrict_z(64, 128, 32 * c) for c in range(4)]

    for copy in copies(0):
        copy.wait()

    def body(i, carry):
        @pl.when(i + 1 < pairs)
        def _():
            for copy in copies(i + 1):
                copy.wait()

        base = 2 * i
        for c in range(4):

            def part(start, step):
                rows = pl.ds(start, step)
                return (buf[c, base, rows] + buf[c, base + 3, rows]) + 3.0 * (
                    buf[c, base + 1, rows] + buf[c, base + 2, rows]
                )

            fill_pad(pad, c, part, NY, 32, NZ)
            restrict_y(pad, c, NY, hi, lo, c * 64, NZ)
        out = dot2(hi[...], lo[...], table)
        for c in range(4):
            v_ref[c, i] = out[c * 64 : c * 64 + 64]
            vbuf[c, i] = out[c * 64 : c * 64 + 64]
        return carry

    lax.fori_loop(0, pairs, body, 0)

    def side(ref, last):
        def row(k):
            return jnp.where(last == 1, ROWS - k, k + 1)

        def vrow(k):
            return jnp.where(last == 1, 7 - k, k)

        r0, r1, r2 = row(0), row(1), row(2)
        for group in range(2):
            for c in range(4):

                def part(start, step):
                    rows = pl.ds(start, step)
                    if group == 0:
                        return buf[c, r0, rows]
                    return 3.0 * (buf[c, r0, rows] + buf[c, r1, rows]) + buf[c, r2, rows]

                fill_pad(pad, c, part, NY, 32, NZ)
                restrict_y(pad, c, NY, hi, lo, c * 64, NZ)
            out = dot2(hi[...], lo[...], table)
            ref[256 * group : 256 * group + 256] = out
        n1, n2 = vrow(1), vrow(2)
        for c in range(4):
            fill_pad(pad2, c, lambda s, t: 3.0 * vbuf[c, n1, pl.ds(s, t)] + vbuf[c, n2, pl.ds(s, t)], 64, 32, 128)
            restrict_y(pad2, c, 64, hi, lo, c * 32, 128)
        for half in range(2):
            at = 64 * half
            ref[512 + 32 * half : 544 + 32 * half] = dot2(
                hi[at : at + 32, 0:128], lo[at : at + 32, 0:128], table_lo
            ) + dot2(hi[at + 32 : at + 64, 0:128], lo[at + 32 : at + 64, 0:128], table_hi)
        m1 = jnp.where(last == 1, 1, 0)
        m2 = jnp.where(last == 1, 0, 1)
        for c in range(4):
            fill_pad(pad3, c, lambda s, t: 3.0 * wbuf[c, m1, pl.ds(s, t)] + wbuf[c, m2, pl.ds(s, t)], 32, 32, 64)
            restrict_y(pad3, c, 32, hi, lo, c * 16, 64)
        total = jnp.zeros((16, 128), F32)
        for c in range(4):
            total = total + dot2(hi[16 * c : 16 * c + 16, 0:64], lo[16 * c : 16 * c + 16, 0:64], table3[c])
        ref[576:592] = total
        classes = jnp.where(last == 1, class_ref[1], class_ref[0]).astype(F32)
        ref[592:608] = jnp.concatenate([classes, jnp.zeros((16, 96), F32)], axis=1)

    table2 = restrict_z(128)
    for m in range(2):
        for c in range(4):
            fill_pad(
                pad2,
                c,
                lambda s, t: (vbuf[c, 2 * m + 1, pl.ds(s, t)] + vbuf[c, 2 * m + 4, pl.ds(s, t)])
                + 3.0 * (vbuf[c, 2 * m + 2, pl.ds(s, t)] + vbuf[c, 2 * m + 3, pl.ds(s, t)]),
                64,
                32,
                128,
            )
            restrict_y(pad2, c, 64, hi, lo, c * 32, 128)
        out = dot2(hi[0:128, 0:128], lo[0:128, 0:128], table2)
        for c in range(4):
            wbuf[c, m] = out[32 * c : 32 * c + 32]
    side(even_ref, 1 - parity)
    side(odd_ref, parity)


def linear_call(void, slip, classes):
    any_spec = pl.BlockSpec(memory_space=pl.ANY)
    vmem = pl.BlockSpec(memory_space=pltpu.VMEM)
    return pl.pallas_call(
        linear_kernel,
        out_shape=(
            jax.ShapeDtypeStruct((4, 8, 64, 128), F32),
            jax.ShapeDtypeStruct((608, 128), F32),
            jax.ShapeDtypeStruct((608, 128), F32),
        ),
        in_specs=[any_spec, any_spec, vmem],
        out_specs=(vmem, vmem, vmem),
        scratch_shapes=[
            pltpu.VMEM((4, ROWS + 2, NY, NZ), F32),
            pltpu.VMEM((8, NY + 16, 128), F32),
            pltpu.VMEM((256, NZ), BF16),
            pltpu.VMEM((256, NZ), BF16),
            pltpu.VMEM((4, 8, 64, 128), F32),
            pltpu.VMEM((4, 2, 32, 64), F32),
            pltpu.VMEM((4, 64 + 16, 128), F32),
            pltpu.VMEM((4, 32 + 16, 128), F32),
            pltpu.SemaphoreType.DMA((8, 2)),
        ],
        compiler_params=pltpu.CompilerParams(vmem_limit_bytes=20 << 20),
        name="linear_part",
    )(void, slip, classes)


def drag_kernel(void_hbm, slip_hbm, class_ref, scale_ref, g_hbm, filt_ref, edge_ref, buf, gbuf, kappa, pad, hi, lo, sems, out_sems):
    pairs = ROWS // 2

    def copies(k):
        rows = pl.ds(2 * k, 2)
        return (
            pltpu.make_async_copy(void_hbm.at[rows], buf.at[0, rows], sems.at[k, 0]),
            pltpu.make_async_copy(slip_hbm.at[:, rows], buf.at[pl.ds(1, 3), rows], sems.at[k, 1]),
        )

    def out_copy(k):
        return pltpu.make_async_copy(gbuf.at[:, pl.ds(2 * k + 1, 2)], g_hbm.at[:, pl.ds(2 * k, 2)], out_sems.at[k])

    for k in range(pairs):
        for copy in copies(k):
            copy.start()
    for c in range(3):
        for row in (0, ROWS + 1):
            for start in range(0, NY, 32):
                gbuf[c, row, start : start + 32] = jnp.zeros((32, NZ), F32)
    for b in range(2):
        kappa[b] = class_factor(scale_ref, spread(class_ref[b].astype(F32), 16, NZ))
    table = restrict_z(NZ)

    def drag_rows(k):
        for copy in copies(k):
            copy.wait()
        block = k // 4
        for row in range(2):
            x = 2 * k + row
            for y in range(16):
                rows = slice(8 * y, 8 * y + 8)
                factor = jnp.broadcast_to(kappa[block, y : y + 1, :], (8, NZ))
                g = drag(buf[0, x, rows], buf[1, x, rows], buf[2, x, rows], buf[3, x, rows], factor)
                for c in range(3):
                    gbuf[c, x + 1, rows] = g[c]
        out_copy(k).start()

    drag_rows(0)

    def body(i, carry):
        @pl.when(i + 1 < pairs)
        def _():
            drag_rows(i + 1)

        base = 2 * i
        for c in range(3):

            def part(start, step):
                rows = pl.ds(start, step)
                return (gbuf[c, base, rows] + gbuf[c, base + 3, rows]) + 3.0 * (
                    gbuf[c, base + 1, rows] + gbuf[c, base + 2, rows]
                )

            fill_pad(pad, c, part, NY, 32, NZ)
            restrict_y(pad, c, NY, hi, lo, c * 64, NZ)
        out = dot2(hi[...], lo[...], table)
        for c in range(3):
            filt_ref[c, i] = out[c * 64 : c * 64 + 64]
        return carry

    lax.fori_loop(0, pairs, body, 0)
    for e, row in enumerate((1, ROWS)):
        for c in range(3):
            fill_pad(pad, c, lambda s, t: gbuf[c, row, pl.ds(s, t)], NY, 32, NZ)
            restrict_y(pad, c, NY, hi, lo, c * 64, NZ)
        out = dot2(hi[...], lo[...], table)
        for c in range(3):
            edge_ref[e, c] = out[c * 64 : c * 64 + 64]
    for k in range(pairs):
        out_copy(k).wait()


def drag_call(void, slip, classes, scale):
    any_spec = pl.BlockSpec(memory_space=pl.ANY)
    vmem = pl.BlockSpec(memory_space=pltpu.VMEM)
    return pl.pallas_call(
        drag_kernel,
        out_shape=(
            jax.ShapeDtypeStruct((3, ROWS, NY, NZ), F32),
            jax.ShapeDtypeStruct((3, 8, 64, 128), F32),
            jax.ShapeDtypeStruct((2, 3, 64, 128), F32),
        ),
        in_specs=[any_spec, any_spec, vmem, pl.BlockSpec(memory_space=pltpu.SMEM)],
        out_specs=(any_spec, vmem, vmem),
        scratch_shapes=[
            pltpu.VMEM((4, ROWS, NY, NZ), F32),
            pltpu.VMEM((3, ROWS + 2, NY, NZ), F32),
            pltpu.VMEM((2, 16, NZ), F32),
            pltpu.VMEM((6, NY + 16, 128), F32),
            pltpu.VMEM((192, NZ), BF16),
            pltpu.VMEM((192, NZ), BF16),
            pltpu.SemaphoreType.DMA((8, 2)),
            pltpu.SemaphoreType.DMA((8,)),
        ],
        compiler_params=pltpu.CompilerParams(vmem_limit_bytes=24 << 20),
        cost_estimate=pl.CostEstimate(flops=60_000_000, bytes_accessed=16_000_000, transcendentals=1_500_000),
        name="drag_part",
    )(void, slip, classes, scale)


def levels_kernel(
    v_in, even_own, odd_own, even_in, odd_in, filt_ref, edge_ref, class_ref, scale_ref,
    g1_ref, g2_ref, g3_ref, sums_ref,
    v, w, z, gpad, pad, hi, lo, kap,
):
    parity = lax.axis_index("blk") % 2
    is_even = parity == 0

    def left(rows):
        return jnp.where(is_even, odd_in[rows], even_in[rows])

    def right(rows):
        return jnp.where(is_even, even_in[rows], odd_in[rows])

    def own_first(rows):
        return jnp.where(is_even, odd_own[rows], even_own[rows])

    def own_last(rows):
        return jnp.where(is_even, even_own[rows], odd_own[rows])

    for c in range(4):
        outer = slice(64 * c, 64 * c + 64)
        combined = slice(256 + 64 * c, 256 + 64 * c + 64)
        v[c, 0] = left(combined) + own_first(outer)
        v[c, 1] = v_in[c, 0] + left(outer)
        for i in range(1, 7):
            v[c, i + 1] = v_in[c, i]
        v[c, 8] = v_in[c, 7] + right(outer)
        v[c, 9] = right(combined) + own_last(outer)
    blocks = [
        left(slice(592, 608))[:, 0:32],
        class_ref[0].astype(F32),
        class_ref[1].astype(F32),
        right(slice(592, 608))[:, 0:32],
    ]
    for b in range(4):
        kap[b] = class_factor(scale_ref, spread(blocks[b], 64, 128))
    numerator = jnp.zeros((64, 128), F32)
    denominator = jnp.zeros((64, 128), F32)
    for i in range(10):
        slips = v[1, i], v[2, i], v[3, i]
        g = drag(v[0, i], *slips, kap[(i + 3) // 4])
        for c in range(3):
            g1_ref[c, i] = g[c]
            if i == 0:
                numerator += edge_ref[0, c] * slips[c]
            elif i == 9:
                numerator += edge_ref[1, c] * slips[c]
            else:
                numerator += filt_ref[c, i - 1] * slips[c]
                denominator += g[c] * slips[c]
    sums = [jnp.sum(numerator, axis=0, keepdims=True), jnp.sum(denominator, axis=0, keepdims=True)]

    table2 = restrict_z(128)

    def x_part(src, c, i, count):
        def part(start, step):
            rows = pl.ds(start, step)
            if i == -1:
                return 3.0 * src[c, 0, rows] + src[c, 1, rows]
            if i == count:
                return src[c, 2 * count, rows] + 3.0 * src[c, 2 * count + 1, rows]
            return (src[c, 2 * i, rows] + src[c, 2 * i + 3, rows]) + 3.0 * (
                src[c, 2 * i + 1, rows] + src[c, 2 * i + 2, rows]
            )

        return part

    n = 0
    for i in range(-1, 5):
        for c in range(4):
            fill_pad(pad, n, x_part(v, c, i, 4), 64, 32, 128)
            restrict_y(pad, n, 64, hi, lo, 32 * n, 128)
            n += 1
    for i in range(4):
        for c in range(3):
            fill_pad(pad, n, x_part(g1_ref, c, i, 4), 64, 32, 128)
            restrict_y(pad, n, 64, hi, lo, 32 * n, 128)
            n += 1
    out = dot2(hi[0 : 32 * n, 0:128], lo[0 : 32 * n, 0:128], table2)
    for i in range(6):
        for c in range(4):
            value = out[32 * (4 * i + c) : 32 * (4 * i + c) + 32]
            if i == 0 or i == 5:
                rows = slice(512 + 32 * (c // 2), 544 + 32 * (c // 2))
                beyond = left(rows) if i == 0 else right(rows)
                if c % 2:
                    beyond = pltpu.roll(beyond, 64, 1)
                value = value + beyond[:, 0:64]
            w[c, i] = value
    numerator = jnp.zeros((32, 64), F32)
    denominator = jnp.zeros((32, 64), F32)
    factors = [class_factor(scale_ref, spread(block, 32, 64)) for block in blocks]
    for i in range(6):
        slips = w[1, i], w[2, i], w[3, i]
        g = drag(w[0, i], *slips, factors[(i + 1) // 2])
        for c in range(3):
            g2_ref[c, i] = g[c]
            if 1 <= i <= 4:
                at = 32 * (24 + 3 * (i - 1) + c)
                numerator += out[at : at + 32] * slips[c]
                denominator += g[c] * slips[c]
    sums += [jnp.sum(numerator, axis=0, keepdims=True), jnp.sum(denominator, axis=0, keepdims=True)]

    table3 = restrict_z(64)
    n = 0
    for i in range(-1, 3):
        for c in range(4):
            fill_pad(gpad, n, x_part(w, c, i, 2), 32, 32, 64)
            restrict_y(gpad, n, 32, hi, lo, 16 * n, 64)
            n += 1
    for i in range(2):
        for c in range(3):
            fill_pad(gpad, n, x_part(g2_ref, c, i, 2), 32, 32, 64)
            restrict_y(gpad, n, 32, hi, lo, 16 * n, 64)
            n += 1
    out = dot2(hi[0 : 16 * n, 0:64], lo[0 : 16 * n, 0:64], table3)
    numerator = jnp.zeros((16, 32), F32)
    denominator = jnp.zeros((16, 32), F32)
    for i in range(4):
        channels = []
        for c in range(4):
            value = out[16 * (4 * i + c) : 16 * (4 * i + c) + 16]
            if i == 0 or i == 3:
                beyond = left(slice(576, 592)) if i == 0 else right(slice(576, 592))
                if c:
                    beyond = pltpu.roll(beyond, 128 - 32 * c, 1)
                value = value + beyond[:, 0:32]
            channels.append(value)
        g = drag(*channels, class_factor(scale_ref, blocks[i]))
        for c in range(3):
            g3_ref[c, i] = g[c]
            if 1 <= i <= 2:
                at = 16 * (16 + 3 * (i - 1) + c)
                numerator += out[at : at + 16] * channels[c + 1]
                denominator += g[c] * channels[c + 1]
    sums += [jnp.sum(numerator, axis=0, keepdims=True), jnp.sum(denominator, axis=0, keepdims=True)]
    wide = [
        part if part.shape[1] == 128 else jnp.concatenate([part, jnp.zeros((1, 128 - part.shape[1]), F32)], axis=1)
        for part in sums
    ]
    tile = jnp.concatenate(wide + [jnp.zeros((2, 128), F32)], axis=0)
    for d in range(16):
        sums_ref[d] = tile


def levels_call(v_part, even_own, odd_own, even_in, odd_in, filt, edge, classes, scale):
    vmem = pl.BlockSpec(memory_space=pltpu.VMEM)
    return pl.pallas_call(
        levels_kernel,
        out_shape=(
            jax.ShapeDtypeStruct((3, 10, 64, 128), F32),
            jax.ShapeDtypeStruct((3, 6, 32, 64), F32),
            jax.ShapeDtypeStruct((3, 4, 16, 32), F32),
            jax.ShapeDtypeStruct((16, 8, 128), F32),
        ),
        in_specs=[vmem] * 8 + [pl.BlockSpec(memory_space=pltpu.SMEM)],
        out_specs=(vmem,) * 4,
        scratch_shapes=[
            pltpu.VMEM((4, 10, 64, 128), F32),
            pltpu.VMEM((4, 6, 32, 64), F32),
            pltpu.VMEM((4, 4, 16, 32), F32),
            pltpu.VMEM((22, 32 + 16, 128), F32),
            pltpu.VMEM((36, 64 + 16, 128), F32),
            pltpu.VMEM((36 * 32, 128), BF16),
            pltpu.VMEM((36 * 32, 128), BF16),
            pltpu.VMEM((4, 64, 128), F32),
        ],
        compiler_params=pltpu.CompilerParams(vmem_limit_bytes=16 << 20),
        name="small_levels",
    )(v_part, even_own, odd_own, even_in, odd_in, filt, edge, classes, scale)


def final_kernel(sums_ref, g1_ref, g2_ref, g3_ref, g0_ref, out_ref, c1, wide3, wide2, pad3, pad2, pad1, wide1, hi, lo, fine, table):
    step = pl.program_id(0)

    def prolong_rows(count, scaled, rows, lanes, pad, wide, z_table):
        for p in range(count):
            pad[p, LEAD : LEAD + rows, 0:lanes] = scaled(p)
            wrap_rows(pad, p, rows)
            prolong_y(pad, p, rows, wide, p)
            split_store(wide[p][:, 0:lanes], hi, lo, 2 * rows * p)
        total = 2 * rows * count
        return dot2(hi[0:total, 0:lanes], lo[0:total, 0:lanes], z_table)

    def make_fine(e):
        values = prolong_rows(3, lambda c: c1[c, e], 64, 128, pad1, wide1, table[...])
        for c in range(3):
            fine[e % 4, c] = values[128 * c : 128 * c + 128]

    @pl.when(step == 0)
    def _():
        table[...] = prolong_z(128)
        total = jnp.sum(sums_ref[...], axis=0)
        r1 = total[0:1] / total[1:2] - 1.0
        r2 = total[2:3, 0:64] / total[3:4, 0:64] - 1.0
        r3 = total[4:5, 0:32] / total[5:6, 0:32] - 1.0

        def x_prolong(planes, count, rows, c):
            for f in range(-1, 2 * count + 1):
                centre = (f >> 1) + 1
                beside = centre + (1 if f & 1 else -1)
                yield f + 1, 3.0 * planes(c, centre) + planes(c, beside)

        up = prolong_rows(12, lambda p: r3 * g3_ref[p // 4, p % 4], 16, 32, pad3, wide3, prolong_z(32))
        c2 = {}
        for c in range(3):
            for f, value in x_prolong(lambda c, e: up[32 * (4 * c + e) : 32 * (4 * c + e) + 32], 2, 32, c):
                c2[c, f] = value + r2 * g2_ref[c, f]
        up2 = prolong_rows(18, lambda p: c2[p // 6, p % 6], 32, 64, pad2, wide2, prolong_z(64))
        for c in range(3):
            for f, value in x_prolong(lambda c, e: up2[64 * (6 * c + e) : 64 * (6 * c + e) + 64], 4, 64, c):
                c1[c, f] = value + r1 * g1_ref[c, f]
        make_fine(0)
        make_fine(1)

    make_fine(step + 2)
    behind, here, ahead = step % 4, (step + 1) % 4, (step + 2) % 4
    for c in range(3):
        for start in range(0, NY, 16):
            rows = slice(start, start + 16)
            centre = 3.0 * fine[here, c, rows]
            out_ref[c, 0, rows] = g0_ref[c, 0, rows] + (centre + fine[behind, c, rows])
            out_ref[c, 1, rows] = g0_ref[c, 1, rows] + (centre + fine[ahead, c, rows])


def final_call(sums, g1, g2, g3, g0):
    def whole(shape):
        return pl.BlockSpec(shape, lambda i: (0,) * len(shape))

    rows = pl.BlockSpec((3, 2, NY, NZ), lambda i: (0, i, 0, 0))
    return pl.pallas_call(
        final_kernel,
        grid=(8,),
        out_shape=jax.ShapeDtypeStruct((3, ROWS, NY, NZ), F32),
        in_specs=[whole((16, 8, 128)), whole((3, 10, 64, 128)), whole((3, 6, 32, 64)), whole((3, 4, 16, 32)), rows],
        out_specs=rows,
        scratch_shapes=[
            pltpu.VMEM((3, 10, 64, 128), F32),
            pltpu.VMEM((12, 32, 128), F32),
            pltpu.VMEM((18, 64, 128), F32),
            pltpu.VMEM((12, 16 + 16, 128), F32),
            pltpu.VMEM((18, 32 + 16, 128), F32),
            pltpu.VMEM((3, 64 + 16, 128), F32),
            pltpu.VMEM((3, 128, 128), F32),
            pltpu.VMEM((18 * 64, 128), BF16),
            pltpu.VMEM((18 * 64, 128), BF16),
            pltpu.VMEM((4, 3, NY, NZ), F32),
            pltpu.VMEM((128, 256), BF16),
        ],
        compiler_params=pltpu.CompilerParams(vmem_limit_bytes=20 << 20),
        name="final_part",
    )(sums, g1, g2, g3, g0)


def shards(void_fraction, slip_velocity, size_class, class_scale):
    count = lax.axis_size("blk")
    even_pairs = [(i, i ^ 1) for i in range(count)]
    odd_pairs = [(i, (i + 1) % count if i % 2 else (i - 1) % count) for i in range(count)]
    v_part, even_own, odd_own = linear_call(void_fraction, slip_velocity, size_class)
    even_in = lax.ppermute(even_own, "blk", even_pairs)
    odd_in = lax.ppermute(odd_own, "blk", odd_pairs)
    g0, filt, edge = drag_call(void_fraction, slip_velocity, size_class, class_scale)
    g1, g2, g3, sums = levels_call(
        v_part, even_own, odd_own, even_in, odd_in, filt, edge, size_class, class_scale
    )
    sums = lax.all_to_all(sums, "blk", 0, 0)
    return final_call(sums, g1, g2, g3, g0)


def solution(mesh):
    return jax.shard_map(
        shards,
        mesh=mesh,
        in_specs=(P("blk", None, "grp"), P(None, "blk", None, "grp"), P("blk", None, "grp"), P()),
        out_specs=P(None, "blk", None, "grp"),
        check_vma=False,
    )
```

time: 207 us -> 48.7 us (0.24)
  local copies, waits for them, and re-layouts: 59.2 us -> 5.1 us
  blocking collectives: 40.8 us -> 13.2 us
  matrix products: 27.5 us -> 0 us
  other arithmetic: 27 us -> 0 us
  starting transfers between devices: 33.9 us -> 7.25 us
  Pallas kernels: 0 us -> 22.9 us
  waiting for transfers between devices: 16.8 us -> 0.01 us
    psum x1 -> x0, blocking collectives: 40.8 us -> none  [shards(): lax.psum((terms_three[0], terms_three[1]), 'blk')]
    reshape x3 -> x0, local copies, waits for them, and re-layouts: 36.6 us -> none  [expand_blocks(): widened.reshape(extent_x * repeat_count, extent_y * repeat_count, extent_...]
    dot_general x12 -> x0, matrix products: 27.5 us -> none  [the longest x6 15.5 us: along_second(): jnp.einsum('cxyz,yw->cxwz', values, table, precision=lax.Precision.HIGHEST)]
    ppermute x12 -> x2, starting transfers between devices: 33.9 us -> 7.25 us  [the longest x1 5.57 us: shards(): odd_in = lax.ppermute(odd_own, 'blk', odd_pairs)]
    pallas_call x0 -> x4, Pallas kernels: none -> 22.9 us  [the longest x1 7.75 us: drag_call(): pl.pallas_call(drag_kernel, out_shape=(jax.ShapeDtypeStruct((3, ROWS, NY,...]
    concatenate x8 -> x0, other arithmetic: 18.8 us -> none  [the longest x3 12.4 us: with_halo(): block = jnp.concatenate([low, block, high], axis=dim)]
    broadcast_in_dim x3 -> x0, local copies, waits for them, and re-layouts: 17.5 us -> none  [expand_blocks(): jnp.broadcast_to(block_values[:, None, :, None, :, None], (extent_x, repe...]
    ppermute x12 -> x2, waiting for transfers between devices: 16.8 us -> 0.01 us  [the longest x1 0.01 us: shards(): even_in = lax.ppermute(even_own, 'blk', even_pairs)]
  transfers between devices with their start and end apart: 12 -> 2, of which waited for: 6 -> 0; matrix products, arithmetic and copies ran while one was open for 9% -> 0% of each run, Pallas kernels for 0% -> 16%
where the time goes in v1:
time: 48.7 us; the launch traced here: 48.5 us
  Pallas kernels  22.9 us (47%)
  blocking collectives  13.2 us (27%)
  starting transfers between devices  7.25 us (15%)
  local copies, waits for them, and re-layouts  5.1 us (10%)
    all_to_all x1, blocking collectives, shards(): sums = lax.all_to_all(sums, 'blk', 0, 0)  13.2 us
    pallas_call x1, Pallas kernels, drag_call(): pl.pallas_call(drag_kernel, out_shape=(jax.ShapeDtypeStruct((3, ROWS, NY,...  7.75 us
    pallas_call x1, Pallas kernels, final_call(): pl.pallas_call(final_kernel, grid=(8,), out_shape=jax.ShapeDtypeStruct((3...  6.94 us
    pallas_call x1, Pallas kernels, linear_call(): pl.pallas_call(linear_kernel, out_shape=(jax.ShapeDtypeStruct((4, 8, 64,...  5.72 us
    ppermute x1, starting transfers between devices, shards(): odd_in = lax.ppermute(odd_own, 'blk', odd_pairs)  5.57 us
    unnamed x12, local copies, waits for them, and re-layouts  5.1 us
    pallas_call x1, Pallas kernels, levels_call(): pl.pallas_call(levels_kernel, out_shape=(jax.ShapeDtypeStruct((3, 10, 64,...  2.45 us
    ppermute x1, starting transfers between devices, shards(): even_in = lax.ppermute(even_own, 'blk', even_pairs)  1.68 us
  transfers between devices with their start and end apart: 2, of which 0 were waited for; matrix products, arithmetic and copies ran while one was open for 0% of the time, Pallas kernels for 16%

profile of v1, /device:TPU:0, one launch (start us, length us, event | category | flops | bytes accessed | tf_op | source)
XLA Modules:
  0.0 48.5 jit_solution(12994020364340591512)
XLA Ops:
  0.0 0.0 copy-start
  0.0 2.8 %copy-done = f32[3,16,128,256]{3,2,1,0:T(8,128)S(1)} copy-done((f32[3,16,128,256]{3,2,1,0:T(8,128)S(1)}, f32[3,16,128,256]{3,2,1,0:T(8,128)}, u32[]{:S(2)}) %copy-start) | copy-done | bytes 6291480
  2.8 0.0 copy-start.2
  2.8 1.6 %copy-done.2 = f32[16,128,256]{2,1,0:T(8,128)S(1)} copy-done((f32[16,128,256]{2,1,0:T(8,128)S(1)}, f32[16,128,256]{2,1,0:T(8,128)}, u32[]{:S(2)}) %copy-start.2) | copy-done | bytes 2097176
  4.4 0.0 copy-start.4
  4.4 0.7 %copy-done.4 = s32[2,16,32]{2,1,0:T(8,128)S(1)} copy-done((s32[2,16,32]{2,1,0:T(8,128)S(1)}, s32[2,16,32]{2,1,0:T(8,128)}, u32[]{:S(2)}) %copy-start.4) | copy-done | bytes 4120
  5.1 0.0 copy-start.1
  5.1 0.0 copy-start.3
  5.1 0.0 copy-start.5
  5.1 5.7 %linear_part.1 = (f32[4,8,64,128]{3,2,1,0:T(8,128)S(1)}, f32[608,128]{1,0:T(8,128)S(1)}, f32[608,128]{1,0:T(8,128)S(1)}) custom-call(f32[16,128,256]{2,1,0:T(8,128)S(1)} %copy-done.2, f32[3,16,128,256]{3,2,1,0:T(8,128)S(1)} %copy-done, s32[2,16,32]{2,1,0:T(8,128)S(1)} %copy-done.4), custom_call_target="tpu_custom_call" | custom-call | tf_op jit(solution)/shard_map/linear_part/pallas_call | solution.py:243
  10.8 1.7 %collective-permute-start = (f32[608,128]{1,0:T(8,128)S(1)}, f32[608,128]{1,0:T(8,128)S(1)}, u32[]{:S(2)}, u32[]{:S(2)}) collective-permute-start(f32[608,128]{1,0:T(8,128)S(1)} %get-tuple-element.16.even_own), channel_id=1, source_target_pairs={{0,1},{1,0},{2,3},{3,2},{4,5},{5,4},{6,7},{7,6},{8,9},{9,8},{10,11... | collective-permute-start | bytes 933896 | tf_op jit(solution)/shard_map/ppermute | solution.py:629
  12.5 5.6 %collective-permute-start.1 = (f32[608,128]{1,0:T(8,128)S(1)}, f32[608,128]{1,0:T(8,128)S(1)}, u32[]{:S(2)}, u32[]{:S(2)}) collective-permute-start(f32[608,128]{1,0:T(8,128)S(1)} %get-tuple-element.17.odd_own), channel_id=1, source_target_pairs={{0,15},{1,2},{2,1},{3,4},{4,3},{5,6},{6,5},{7,8},{8,7},{9,10},{10,... | collective-permute-start | bytes 933896 | tf_op jit(solution)/shard_map/ppermute | solution.py:630
  18.1 0.0 copy-done.1
  18.1 0.0 copy-done.3
  18.1 0.0 copy-done.5
  18.1 7.7 %drag_part.1 = (f32[3,16,128,256]{3,2,1,0:T(8,128)S(1)}, f32[3,8,64,128]{3,2,1,0:T(8,128)S(1)}, f32[2,3,64,128]{3,2,1,0:T(8,128)S(1)}) custom-call(f32[16,128,256]{2,1,0:T(8,128)S(1)} %copy-done.3, f32[3,16,128,256]{3,2,1,0:T(8,128)S(1)} %copy-done.1, s32[2,16,32]{2,1,0:T(8,128)S(1)} %copy-done.4, f32[4]{0:T(128)S(1)} %copy-done.5), custom_call_target="tpu_custom_call" | custom-call | flops 60000000 | bytes 16000000 | tf_op jit(solution)/shard_map/drag_part/pallas_call | solution.py:344
  25.8 0.0 collective-permute-done.even_in
  25.9 0.0 collective-permute-done.1.odd_in
  25.9 2.4 %small_levels.1 = (f32[3,10,64,128]{3,2,1,0:T(8,128)S(1)}, f32[3,6,32,64]{3,2,1,0:T(8,128)S(1)}, f32[3,4,16,32]{3,2,1,0:T(8,128)S(1)}, f32[16,8,128]{2,1,0:T(8,128)S(1)}) custom-call(f32[4,8,64,128]{3,2,1,0:T(8,128)S(1)} %get-tuple-element.15.v_in, f32[608,128]{1,0:T(8,128)S(1)} %get-tuple-element.16.even_own, f32[608,128]{1,0:T(8,128)S(1)} %get-tuple-element.17.odd_own, ...), custom_call_target="tpu_custom_call" | custom-call | tf_op jit(solution)/shard_map/small_levels/pallas_call | solution.py:517
  28.3 13.2 %all_to_all.5.sums_ref = f32[16,8,128]{2,1,0:T(8,128)S(1)} all-to-all(f32[16,8,128]{2,1,0:T(8,128)S(1)} %get-tuple-element.20), channel_id=1, replica_groups=mesh['grp'=8,'blk'=16] {'blk'}, dimensions={0} | all-to-all | bytes 131072 | tf_op jit(solution)/shard_map/all_to_all | solution.py:635
  41.5 6.9 %final_part.1 = f32[3,16,128,256]{3,2,1,0:T(8,128)} custom-call(f32[16,8,128]{2,1,0:T(8,128)S(1)} %all_to_all.5.sums_ref, f32[3,10,64,128]{3,2,1,0:T(8,128)S(1)} %get-tuple-element.21.g1_ref, f32[3,6,32,64]{3,2,1,0:T(8,128)S(1)} %get-tuple-element.22.g2_ref, f32[3,4,16,32]{3,2,1,0:T(8,128)S(1)} %get-tuple-element.23.g3_ref, ...), custom_call_target="tpu_custom_call" | custom-call | tf_op jit(solution)/shard_map/final_part/pallas_call | solution.py:600
Async XLA Ops:
  0.0 2.8 %copy-start = (f32[3,16,128,256]{3,2,1,0:T(8,128)S(1)}, f32[3,16,128,256]{3,2,1,0:T(8,128)}, u32[]{:S(2)}) copy-start(f32[3,16,128,256]{3,2,1,0:T(8,128)} %slip_hbm.3) | copy-start | bytes 18874372
  2.8 1.6 %copy-start.2 = (f32[16,128,256]{2,1,0:T(8,128)S(1)}, f32[16,128,256]{2,1,0:T(8,128)}, u32[]{:S(2)}) copy-start(f32[16,128,256]{2,1,0:T(8,128)} %void_hbm.3) | copy-start | bytes 6291460
  4.4 0.7 %copy-start.4 = (s32[2,16,32]{2,1,0:T(8,128)S(1)}, s32[2,16,32]{2,1,0:T(8,128)}, u32[]{:S(2)}) copy-start(s32[2,16,32]{2,1,0:T(8,128)} %class_ref.5) | copy-start | bytes 12292
  5.1 13.0 %copy-start.1 = (f32[3,16,128,256]{3,2,1,0:T(8,128)S(1)}, f32[3,16,128,256]{3,2,1,0:T(8,128)}, u32[]{:S(2)}) copy-start(f32[3,16,128,256]{3,2,1,0:T(8,128)} %slip_hbm.3) | copy-start | bytes 18874372
  5.1 13.0 %copy-start.3 = (f32[16,128,256]{2,1,0:T(8,128)S(1)}, f32[16,128,256]{2,1,0:T(8,128)}, u32[]{:S(2)}) copy-start(f32[16,128,256]{2,1,0:T(8,128)} %void_hbm.3) | copy-start | bytes 6291460
  5.1 13.0 %copy-start.5 = (f32[4]{0:T(128)S(1)}, f32[4]{0:T(128)}, u32[]{:S(2)}) copy-start(f32[4]{0:T(128)} %scale_ref.3) | copy-start | bytes 52
  10.8 15.0 %collective-permute-start = (f32[608,128]{1,0:T(8,128)S(1)}, f32[608,128]{1,0:T(8,128)S(1)}, u32[]{:S(2)}, u32[]{:S(2)}) collective-permute-start(f32[608,128]{1,0:T(8,128)S(1)} %get-tuple-element.16.even_own), channel_id=1, source_target_pairs={{0,1},{1,0},{2,3},{3,2},{4,5},{5,4},{6,7},{7,6},{8,9},{9,8},{10,11... | collective-permute-start | bytes 933896 | tf_op jit(solution)/shard_map/ppermute | solution.py:629
  12.5 13.3 %collective-permute-start.1 = (f32[608,128]{1,0:T(8,128)S(1)}, f32[608,128]{1,0:T(8,128)S(1)}, u32[]{:S(2)}, u32[]{:S(2)}) collective-permute-start(f32[608,128]{1,0:T(8,128)S(1)} %get-tuple-element.17.odd_own), channel_id=1, source_target_pairs={{0,15},{1,2},{2,1},{3,4},{4,3},{5,6},{6,5},{7,8},{8,7},{9,10},{10,... | collective-permute-start | bytes 933896 | tf_op jit(solution)/shard_map/ppermute | solution.py:630

commit v2 on v1

v2 whole, which is shorter than its diff:
```python
import math

import jax
import jax.numpy as jnp
from jax import lax
from jax.experimental import pallas as pl
from jax.experimental.pallas import tpu as pltpu
from jax.sharding import PartitionSpec as P

F32 = jnp.float32
BF16 = jnp.bfloat16
ROWS = 16
NY = 128
NZ = 256
LEAD = 8
TINY = 1.1754944e-38
POWER = -1.65 * math.log2(math.e)


def iota(shape, axis):
    return lax.broadcasted_iota(jnp.int32, shape, axis)


def restrict_z(length, width=None, shift=0):
    width = width or length // 2
    fine = iota((length, width), 0)
    coarse = iota((length, width), 1) - shift
    offset = fine - 2 * coarse
    weight = jnp.where((offset == 0) | (offset == 1), 3.0, 0.0)
    weight = weight + jnp.where((offset == -1) | (offset == 2), 1.0, 0.0)
    weight = weight + jnp.where((fine == 0) & (coarse == 0), 1.0, 0.0)
    last = length // 2 - 1
    weight = weight + jnp.where((fine == length - 1) & (coarse == last), 1.0, 0.0)
    weight = jnp.where((coarse >= 0) & (coarse <= last), weight, 0.0)
    return (weight * (1.0 / 512.0)).astype(BF16)


def spread(values, rows, lanes):
    a, b = values.shape
    along = (iota((b, lanes), 0) == iota((b, lanes), 1) // (lanes // b)).astype(BF16)
    wide = jnp.dot(values.astype(BF16), along, preferred_element_type=F32)
    if rows == a:
        return wide
    down = (iota((rows, a), 1) == iota((rows, a), 0) // (rows // a)).astype(BF16)
    return jnp.dot(down, wide.astype(BF16), preferred_element_type=F32)


def class_factor(scale_ref, classes):
    chosen = jnp.where(classes < 0.5, scale_ref[0], scale_ref[1])
    chosen = jnp.where(classes < 1.5, chosen, scale_ref[2])
    return jnp.where(classes < 2.5, chosen, scale_ref[3])


def drag(void, s0, s1, s2, kappa):
    square = s0 * s0 + s1 * s1 + s2 * s2
    speed = square * lax.rsqrt(jnp.maximum(square, TINY))
    factor = (kappa * (1.0 - void)) * (jnp.exp2(POWER * jnp.log(void)) * speed)
    return factor * s0, factor * s1, factor * s2


def dot2(hi, lo, table):
    return jnp.dot(hi, table, preferred_element_type=F32) + jnp.dot(
        lo, table, preferred_element_type=F32
    )


def wrap_rows(pad, q, rows):
    pad[q, LEAD - 1 : LEAD] = pad[q, LEAD + rows - 1 : LEAD + rows]
    pad[q, LEAD + rows : LEAD + rows + 1] = pad[q, LEAD : LEAD + 1]


def fill_pad(pad, p, part, rows, step, lanes):
    planes = -(-lanes // 128)
    for start in range(0, rows, step):
        value = part(start, step)
        rng = slice(LEAD + start, LEAD + start + step)
        if lanes < 128:
            pad[p, rng, 0:lanes] = value
        else:
            for h in range(planes):
                pad[planes * p + h, rng] = value[:, 128 * h : 128 * h + 128]
    for h in range(planes):
        wrap_rows(pad, planes * p + h, rows)


def restrict_y(pad, p, rows, hi_ref, lo_ref, out_start, lanes, step=16):
    half = rows // 2
    step = min(step, half)
    planes = -(-lanes // 128)
    width = min(lanes, 128)
    for start in range(0, half, step):
        for h in range(planes):
            at = LEAD + 2 * start
            q = planes * p + h
            outer = pad[q, pl.ds(at - 1, step, stride=2), :] + pad[q, pl.ds(at + 2, step, stride=2), :]
            inner = pad[q, pl.ds(at, step, stride=2), :] + pad[q, pl.ds(at + 1, step, stride=2), :]
            value = (outer + 3.0 * inner)[:, 0:width]
            hi = value.astype(BF16)
            rng = slice(out_start + start, out_start + start + step)
            cols = slice(128 * h, 128 * h + width)
            hi_ref[rng, cols] = hi
            lo_ref[rng, cols] = (value - hi.astype(F32)).astype(BF16)


def prolong_y(pad, p, rows, wide, q):
    step = min(rows, 32)
    for start in range(0, rows, step):
        at = LEAD + start
        centre = 3.0 * pad[p, at : at + step]
        wide[q, pl.ds(2 * start, step, stride=2), :] = centre + pad[p, at - 1 : at - 1 + step]
        wide[q, pl.ds(2 * start + 1, step, stride=2), :] = centre + pad[p, at + 1 : at + 1 + step]


def y_rows(src, lead, dst, half_rows):
    for start in range(0, half_rows, 16):
        for h in range(2):
            at = lead + 2 * start
            plane = src(h)
            outer = plane[pl.ds(at - 1, 16, stride=2), :] + plane[pl.ds(at + 2, 16, stride=2), :]
            inner = plane[pl.ds(at, 16, stride=2), :] + plane[pl.ds(at + 1, 16, stride=2), :]
            dst(h, start, outer + 3.0 * inner)


def split_at(value, hi, lo, row, col):
    top = value.astype(BF16)
    rows = slice(row, row + value.shape[0])
    cols = slice(col, col + value.shape[1])
    hi[rows, cols] = top
    lo[rows, cols] = (value - top.astype(F32)).astype(BF16)


def x_rows(ybuf, c, rows, weights, hi, lo, at):
    for start in range(0, 64, 16):
        for h in range(2):
            parts = [ybuf[c, r, h, start : start + 16] for r in rows]
            ones = [p for p, w in zip(parts, weights) if w == 1]
            threes = [p for p, w in zip(parts, weights) if w == 3]
            value = sum(ones[1:], ones[0]) if ones else None
            if threes:
                heavy = 3.0 * sum(threes[1:], threes[0])
                value = heavy if value is None else value + heavy
            split_at(value, hi, lo, at + start, 128 * h)


def linear_kernel(void_hbm, slip_hbm, class_hbm, v_ref, even_ref, odd_ref, fields, class_ref, ybuf, hi, lo, wbuf, pad2, pad3, classes, sems, class_sem):
    parity = lax.axis_index("blk") % 2
    pairs = ROWS // 2

    def copies(k):
        rows = pl.ds(2 * k, 2)
        y = pl.ds(LEAD, NY)
        out = []
        for h in range(2):
            z = pl.ds(128 * h, 128)
            out.append(pltpu.make_async_copy(void_hbm.at[rows, :, z], fields.at[0, rows, h, y], sems.at[k, h]))
            out.append(pltpu.make_async_copy(slip_hbm.at[:, rows, :, z], fields.at[pl.ds(1, 3), rows, h, y], sems.at[k, 2 + h]))
        return out

    class_copy = pltpu.make_async_copy(class_hbm, classes, class_sem)
    class_copy.start()
    for k in range(pairs):
        for copy in copies(k):
            copy.start()
    for c in range(4):
        for row in (0, ROWS + 1):
            for h in range(2):
                ybuf[c, row, h] = jnp.zeros((64, 128), F32)
    table = restrict_z(NZ)
    table_lo = restrict_z(128, 128, 0)
    table_hi = restrict_z(128, 128, 64)
    table3 = [restrict_z(64, 128, 32 * c) for c in range(4)]
    class_copy.wait()
    class_ref[...] = classes[...].astype(F32)

    def along_y(k):
        for copy in copies(k):
            copy.wait()
        for c in range(4):
            for r in range(2):
                row = 2 * k + r
                for h in range(2):
                    wrap_plane(fields, (c, row, h), NY)

                def put(h, start, value):
                    ybuf[c, row + 1, h, start : start + 16] = value

                y_rows(lambda h: fields.at[c, row, h], LEAD, put, 64)

    def along_x(i, at):
        base = 2 * i
        for c in range(4):
            x_rows(ybuf, c, (base, base + 1, base + 2, base + 3), (1, 3, 3, 1), hi, lo, at + 64 * c)
        out = dot2(hi[at : at + 256], lo[at : at + 256], table)
        for c in range(4):
            v_ref[c, i] = out[c * 64 : c * 64 + 64]

    along_y(0)

    def body(i, carry):
        along_y(i + 1)
        along_x(i, 0)
        return carry

    lax.fori_loop(0, pairs - 1, body, 0)
    along_x(pairs - 1, 0)

    def side_rows(ref, last, at):
        r0 = jnp.where(last == 1, ROWS, 1)
        r1 = jnp.where(last == 1, ROWS - 1, 2)
        r2 = jnp.where(last == 1, ROWS - 2, 3)
        for c in range(4):
            x_rows(ybuf, c, (r0,), (1,), hi, lo, at + 64 * c)
            x_rows(ybuf, c, (r0, r1, r2), (3, 3, 1), hi, lo, at + 256 + 64 * c)
        ref[0:512] = dot2(hi[at : at + 512], lo[at : at + 512], table)

    side_rows(even_ref, 1 - parity, 256)
    side_rows(odd_ref, parity, 768)

    table2 = restrict_z(128)
    for m in range(2):
        for c in range(4):
            fill_pad(
                pad2,
                4 * m + c,
                lambda s, t: (v_ref[c, 2 * m + 1, pl.ds(s, t)] + v_ref[c, 2 * m + 4, pl.ds(s, t)])
                + 3.0 * (v_ref[c, 2 * m + 2, pl.ds(s, t)] + v_ref[c, 2 * m + 3, pl.ds(s, t)]),
                64,
                32,
                128,
            )
            restrict_y(pad2, 4 * m + c, 64, hi, lo, 32 * (4 * m + c), 128)
    out = dot2(hi[0:256, 0:128], lo[0:256, 0:128], table2)
    for m in range(2):
        for c in range(4):
            wbuf[c, m] = out[32 * (4 * m + c) : 32 * (4 * m + c) + 32]

    def side_levels(ref, last, slot):
        n1 = jnp.where(last == 1, 6, 1)
        n2 = jnp.where(last == 1, 5, 2)
        at = 256 + 128 * slot
        for c in range(4):
            p = 8 + 4 * slot + c
            fill_pad(pad2, p, lambda s, t: 3.0 * v_ref[c, n1, pl.ds(s, t)] + v_ref[c, n2, pl.ds(s, t)], 64, 32, 128)
            restrict_y(pad2, p, 64, hi, lo, at + 32 * c, 128)
        for half in range(2):
            row = at + 64 * half
            ref[512 + 32 * half : 544 + 32 * half] = dot2(
                hi[row : row + 32, 0:128], lo[row : row + 32, 0:128], table_lo
            ) + dot2(hi[row + 32 : row + 64, 0:128], lo[row + 32 : row + 64, 0:128], table_hi)
        m1 = jnp.where(last == 1, 1, 0)
        m2 = jnp.where(last == 1, 0, 1)
        at = 512 + 64 * slot
        for c in range(4):
            p = 4 * slot + c
            fill_pad(pad3, p, lambda s, t: 3.0 * wbuf[c, m1, pl.ds(s, t)] + wbuf[c, m2, pl.ds(s, t)], 32, 32, 64)
            restrict_y(pad3, p, 32, hi, lo, at + 16 * c, 64)
        total = jnp.zeros((16, 128), F32)
        for c in range(4):
            row = at + 16 * c
            total = total + dot2(hi[row : row + 16, 0:64], lo[row : row + 16, 0:64], table3[c])
        ref[576:592] = total
        outer = jnp.where(last == 1, class_ref[1], class_ref[0])
        ref[592:608] = jnp.concatenate([outer, jnp.zeros((16, 96), F32)], axis=1)

    side_levels(even_ref, 1 - parity, 0)
    side_levels(odd_ref, parity, 1)


def wrap_plane(ref, index, rows):
    plane = ref.at[index]
    plane[LEAD - 1 : LEAD] = plane[LEAD + rows - 1 : LEAD + rows]
    plane[LEAD + rows : LEAD + rows + 1] = plane[LEAD : LEAD + 1]


def linear_call(void, slip, classes):
    hbm = pl.BlockSpec(memory_space=pltpu.HBM)
    vmem = pl.BlockSpec(memory_space=pltpu.VMEM)
    return pl.pallas_call(
        linear_kernel,
        out_shape=(
            jax.ShapeDtypeStruct((4, 8, 64, 128), F32),
            jax.ShapeDtypeStruct((608, 128), F32),
            jax.ShapeDtypeStruct((608, 128), F32),
            jax.ShapeDtypeStruct((4, ROWS, 2, NY + 16, 128), F32),
            jax.ShapeDtypeStruct((2, 16, 32), F32),
        ),
        in_specs=[hbm, hbm, hbm],
        out_specs=(vmem,) * 5,
        scratch_shapes=[
            pltpu.VMEM((4, ROWS + 2, 2, 64, 128), F32),
            pltpu.VMEM((1280, NZ), BF16),
            pltpu.VMEM((1280, NZ), BF16),
            pltpu.VMEM((4, 2, 32, 64), F32),
            pltpu.VMEM((16, 64 + 16, 128), F32),
            pltpu.VMEM((8, 32 + 16, 128), F32),
            pltpu.VMEM((2, 16, 32), jnp.int32),
            pltpu.SemaphoreType.DMA((8, 4)),
            pltpu.SemaphoreType.DMA,
        ],
        compiler_params=pltpu.CompilerParams(vmem_limit_bytes=12 << 20),
        name="linear_part",
    )(void, slip, classes)


def drag_kernel(fields, class_ref, scale_ref, g_ref, filt_ref, edge_ref, kappa, ybuf, hi, lo):
    pairs = ROWS // 2
    for c in range(3):
        for row in (0, ROWS + 1):
            for h in range(2):
                ybuf[c, row, h] = jnp.zeros((64, 128), F32)
    for b in range(2):
        kappa[b] = class_factor(scale_ref, spread(class_ref[b], 16, NZ))
    table = restrict_z(NZ)

    def drag_rows(k):
        block = k // 4
        for r in range(2):
            x = 2 * k + r
            for y in range(16):
                rows = slice(LEAD + 8 * y, LEAD + 8 * y + 8)
                for h in range(2):
                    factor = jnp.broadcast_to(kappa[block, y : y + 1, 128 * h : 128 * h + 128], (8, 128))
                    g = drag(*(fields[c, x, h, rows] for c in range(4)), factor)
                    for c in range(3):
                        g_ref[c, x, h, rows] = g[c]
            for c in range(3):
                for h in range(2):
                    wrap_plane(g_ref, (c, x, h), NY)

    def along_y(k):
        for c in range(3):
            for r in range(2):
                row = 2 * k + r

                def put(h, start, value):
                    ybuf[c, row + 1, h, start : start + 16] = value

                y_rows(lambda h: g_ref.at[c, row, h], LEAD, put, 64)

    def along_x(i, at):
        base = 2 * i
        for c in range(3):
            x_rows(ybuf, c, (base, base + 1, base + 2, base + 3), (1, 3, 3, 1), hi, lo, at + 64 * c)
        out = dot2(hi[at : at + 192], lo[at : at + 192], table)
        for c in range(3):
            filt_ref[c, i] = out[c * 64 : c * 64 + 64]

    drag_rows(0)
    drag_rows(1)
    along_y(0)

    def body(i, carry):
        drag_rows(i + 2)
        along_y(i + 1)
        along_x(i, 0)
        return carry

    lax.fori_loop(0, pairs - 2, body, 0)
    along_y(pairs - 1)
    along_x(pairs - 2, 0)
    along_x(pairs - 1, 192)
    for e, row in enumerate((1, ROWS)):
        at = 384 + 192 * e
        for c in range(3):
            x_rows(ybuf, c, (row,), (1,), hi, lo, at + 64 * c)
        out = dot2(hi[at : at + 192], lo[at : at + 192], table)
        for c in range(3):
            edge_ref[e, c] = out[c * 64 : c * 64 + 64]


def drag_call(fields, classes, scale):
    vmem = pl.BlockSpec(memory_space=pltpu.VMEM)
    return pl.pallas_call(
        drag_kernel,
        out_shape=(
            jax.ShapeDtypeStruct((3, ROWS, 2, NY + 16, 128), F32),
            jax.ShapeDtypeStruct((3, 8, 64, 128), F32),
            jax.ShapeDtypeStruct((2, 3, 64, 128), F32),
        ),
        in_specs=[vmem, vmem, pl.BlockSpec(memory_space=pltpu.SMEM)],
        out_specs=(vmem,) * 3,
        scratch_shapes=[
            pltpu.VMEM((2, 16, NZ), F32),
            pltpu.VMEM((3, ROWS + 2, 2, 64, 128), F32),
            pltpu.VMEM((768, NZ), BF16),
            pltpu.VMEM((768, NZ), BF16),
        ],
        compiler_params=pltpu.CompilerParams(vmem_limit_bytes=10 << 20),
        cost_estimate=pl.CostEstimate(flops=60_000_000, bytes_accessed=16_000_000, transcendentals=1_500_000),
        name="drag_part",
    )(fields, classes, scale)


def x_prolong(planes, count):
    for f in range(-1, 2 * count + 1):
        centre = (f >> 1) + 1
        beside = centre + (1 if f & 1 else -1)
        yield f + 1, 3.0 * planes(centre) + planes(beside)


def plain_prolong_z(length):
    coarse = iota((length, 2 * length), 0)
    fine = iota((length, 2 * length), 1)
    centre = lax.shift_right_logical(fine, 1)
    neighbour = jnp.clip(centre - 1 + 2 * (fine & 1), 0, length - 1)
    return (jnp.where(coarse == centre, 3.0, 0.0) + jnp.where(coarse == neighbour, 1.0, 0.0)).astype(BF16)


def prolong_levels(g1_ref, g2_ref, g3_ref, wide_ref, table_ref, pad3, up3, pad2, up2, pad1):
    first = plain_prolong_z(128)
    second = jnp.dot(plain_prolong_z(64), first, preferred_element_type=F32)
    third = jnp.dot(plain_prolong_z(32), plain_prolong_z(64), preferred_element_type=F32)
    third = jnp.dot(third.astype(BF16), first, preferred_element_type=F32)
    table_ref[0:128] = (first.astype(F32) * (1.0 / 64.0)).astype(BF16)
    table_ref[128:192] = (second * (1.0 / 64.0**2)).astype(BF16)
    table_ref[192:224] = (third * (1.0 / 64.0**3)).astype(BF16)
    table_ref[224:256] = jnp.zeros((32, NZ), BF16)
    for c in range(3):
        for e in range(4):
            p = 4 * c + e
            pad3[p, LEAD : LEAD + 16, 0:32] = g3_ref[c, e]
            wrap_rows(pad3, p, 16)
            prolong_y(pad3, p, 16, up3, p)
        for f, value in x_prolong(lambda e: up3[4 * c + e], 2):
            both = jnp.concatenate([g2_ref[c, f], value[:, 0:32], jnp.zeros((32, 32), F32)], axis=1)
            p = 6 * c + f
            pad2[p, LEAD : LEAD + 32] = both
            wrap_rows(pad2, p, 32)
            prolong_y(pad2, p, 32, up2, p)
        for f, value in x_prolong(lambda e: up2[6 * c + e], 4):
            p = 10 * c + f
            for h, part in enumerate((g1_ref[c, f], value)):
                q = 2 * p + h
                pad1[q, LEAD : LEAD + 64] = part
                wrap_rows(pad1, q, 64)
                prolong_y(pad1, q, 64, wide_ref, q)


def levels_kernel(
    v_in, even_own, odd_own, even_in, odd_in, filt_ref, edge_ref, class_ref, scale_ref,
    wide_ref, table_ref, sums_ref,
    v, w, g1_ref, g2_ref, g3_ref, gpad, pad, hi, lo, kap, pad3, up3, pad2, up2, pad1,
):
    parity = lax.axis_index("blk") % 2
    is_even = parity == 0

    def left(rows):
        return jnp.where(is_even, odd_in[rows], even_in[rows])

    def right(rows):
        return jnp.where(is_even, even_in[rows], odd_in[rows])

    def own_first(rows):
        return jnp.where(is_even, odd_own[rows], even_own[rows])

    def own_last(rows):
        return jnp.where(is_even, even_own[rows], odd_own[rows])

    for c in range(4):
        outer = slice(64 * c, 64 * c + 64)
        combined = slice(256 + 64 * c, 256 + 64 * c + 64)
        v[c, 0] = left(combined) + own_first(outer)
        v[c, 1] = v_in[c, 0] + left(outer)
        for i in range(1, 7):
            v[c, i + 1] = v_in[c, i]
        v[c, 8] = v_in[c, 7] + right(outer)
        v[c, 9] = right(combined) + own_last(outer)
    blocks = [
        left(slice(592, 608))[:, 0:32],
        class_ref[0],
        class_ref[1],
        right(slice(592, 608))[:, 0:32],
    ]
    for b in range(4):
        kap[b] = class_factor(scale_ref, spread(blocks[b], 64, 128))
    numerator = jnp.zeros((64, 128), F32)
    denominator = jnp.zeros((64, 128), F32)
    for i in range(10):
        slips = v[1, i], v[2, i], v[3, i]
        g = drag(v[0, i], *slips, kap[(i + 3) // 4])
        for c in range(3):
            g1_ref[c, i] = g[c]
            if i == 0:
                numerator += edge_ref[0, c] * slips[c]
            elif i == 9:
                numerator += edge_ref[1, c] * slips[c]
            else:
                numerator += filt_ref[c, i - 1] * slips[c]
                denominator += g[c] * slips[c]
    sums = [jnp.sum(numerator, axis=0, keepdims=True), jnp.sum(denominator, axis=0, keepdims=True)]

    table2 = restrict_z(128)

    def x_part(src, c, i, count):
        def part(start, step):
            rows = pl.ds(start, step)
            if i == -1:
                return 3.0 * src[c, 0, rows] + src[c, 1, rows]
            if i == count:
                return src[c, 2 * count, rows] + 3.0 * src[c, 2 * count + 1, rows]
            return (src[c, 2 * i, rows] + src[c, 2 * i + 3, rows]) + 3.0 * (
                src[c, 2 * i + 1, rows] + src[c, 2 * i + 2, rows]
            )

        return part

    n = 0
    for i in range(-1, 5):
        for c in range(4):
            fill_pad(pad, n, x_part(v, c, i, 4), 64, 32, 128)
            restrict_y(pad, n, 64, hi, lo, 32 * n, 128)
            n += 1
    for i in range(4):
        for c in range(3):
            fill_pad(pad, n, x_part(g1_ref, c, i, 4), 64, 32, 128)
            restrict_y(pad, n, 64, hi, lo, 32 * n, 128)
            n += 1
    out = dot2(hi[0 : 32 * n, 0:128], lo[0 : 32 * n, 0:128], table2)
    for i in range(6):
        for c in range(4):
            value = out[32 * (4 * i + c) : 32 * (4 * i + c) + 32]
            if i == 0 or i == 5:
                rows = slice(512 + 32 * (c // 2), 544 + 32 * (c // 2))
                beyond = left(rows) if i == 0 else right(rows)
                if c % 2:
                    beyond = pltpu.roll(beyond, 64, 1)
                value = value + beyond[:, 0:64]
            w[c, i] = value
    numerator = jnp.zeros((32, 64), F32)
    denominator = jnp.zeros((32, 64), F32)
    factors = [class_factor(scale_ref, spread(block, 32, 64)) for block in blocks]
    for i in range(6):
        slips = w[1, i], w[2, i], w[3, i]
        g = drag(w[0, i], *slips, factors[(i + 1) // 2])
        for c in range(3):
            g2_ref[c, i] = g[c]
            if 1 <= i <= 4:
                at = 32 * (24 + 3 * (i - 1) + c)
                numerator += out[at : at + 32] * slips[c]
                denominator += g[c] * slips[c]
    sums += [jnp.sum(numerator, axis=0, keepdims=True), jnp.sum(denominator, axis=0, keepdims=True)]

    table3 = restrict_z(64)
    n = 0
    for i in range(-1, 3):
        for c in range(4):
            fill_pad(gpad, n, x_part(w, c, i, 2), 32, 32, 64)
            restrict_y(gpad, n, 32, hi, lo, 16 * n, 64)
            n += 1
    for i in range(2):
        for c in range(3):
            fill_pad(gpad, n, x_part(g2_ref, c, i, 2), 32, 32, 64)
            restrict_y(gpad, n, 32, hi, lo, 16 * n, 64)
            n += 1
    out = dot2(hi[0 : 16 * n, 0:64], lo[0 : 16 * n, 0:64], table3)
    numerator = jnp.zeros((16, 32), F32)
    denominator = jnp.zeros((16, 32), F32)
    for i in range(4):
        channels = []
        for c in range(4):
            value = out[16 * (4 * i + c) : 16 * (4 * i + c) + 16]
            if i == 0 or i == 3:
                beyond = left(slice(576, 592)) if i == 0 else right(slice(576, 592))
                if c:
                    beyond = pltpu.roll(beyond, 128 - 32 * c, 1)
                value = value + beyond[:, 0:32]
            channels.append(value)
        g = drag(*channels, class_factor(scale_ref, blocks[i]))
        for c in range(3):
            g3_ref[c, i] = g[c]
            if 1 <= i <= 2:
                at = 16 * (16 + 3 * (i - 1) + c)
                numerator += out[at : at + 16] * channels[c + 1]
                denominator += g[c] * channels[c + 1]
    sums += [jnp.sum(numerator, axis=0, keepdims=True), jnp.sum(denominator, axis=0, keepdims=True)]
    ones = jnp.ones((1, 32), F32)
    packed = [sums[0], sums[1]] + [jnp.concatenate([sums[2 + k], sums[4 + k], ones], axis=1) for k in range(2)]
    tile = jnp.concatenate(packed + [jnp.zeros((4, 128), F32)], axis=0)
    for d in range(16):
        sums_ref[d] = tile
    prolong_levels(g1_ref, g2_ref, g3_ref, wide_ref, table_ref, pad3, up3, pad2, up2, pad1)


def levels_call(v_part, even_own, odd_own, even_in, odd_in, filt, edge, classes, scale):
    vmem = pl.BlockSpec(memory_space=pltpu.VMEM)
    return pl.pallas_call(
        levels_kernel,
        out_shape=(
            jax.ShapeDtypeStruct((60, NY, 128), F32),
            jax.ShapeDtypeStruct((256, NZ), BF16),
            jax.ShapeDtypeStruct((16, 8, 128), F32),
        ),
        in_specs=[vmem] * 8 + [pl.BlockSpec(memory_space=pltpu.SMEM)],
        out_specs=(vmem,) * 3,
        scratch_shapes=[
            pltpu.VMEM((4, 10, 64, 128), F32),
            pltpu.VMEM((4, 6, 32, 64), F32),
            pltpu.VMEM((3, 10, 64, 128), F32),
            pltpu.VMEM((3, 6, 32, 64), F32),
            pltpu.VMEM((3, 4, 16, 32), F32),
            pltpu.VMEM((22, 32 + 16, 128), F32),
            pltpu.VMEM((36, 64 + 16, 128), F32),
            pltpu.VMEM((36 * 32, 128), BF16),
            pltpu.VMEM((36 * 32, 128), BF16),
            pltpu.VMEM((4, 64, 128), F32),
            pltpu.VMEM((12, 16 + 16, 128), F32),
            pltpu.VMEM((12, 32, 128), F32),
            pltpu.VMEM((18, 32 + 16, 128), F32),
            pltpu.VMEM((18, 64, 128), F32),
            pltpu.VMEM((60, 64 + 16, 128), F32),
        ],
        compiler_params=pltpu.CompilerParams(vmem_limit_bytes=14 << 20),
        name="small_levels",
    )(v_part, even_own, odd_own, even_in, odd_in, filt, edge, classes, scale)


def final_kernel(sums_ref, wide_ref, table_ref, g0_ref, out_hbm, stage, hi, lo, fine, sems):
    total = jnp.sum(sums_ref[...], axis=0)
    ratios = [total[2 * h : 2 * h + 1] / total[2 * h + 1 : 2 * h + 2] - 1.0 for h in range(2)]

    def make_fine(e):
        slot = e % 2
        for c in range(3):
            for h in range(2):
                for start in range(0, NY, 16):
                    value = wide_ref[20 * c + 2 * e + h, start : start + 16] * ratios[h]
                    split_at(value, hi.at[slot], lo.at[slot], NY * c + start, 128 * h)
        for c in range(3):
            rows = slice(NY * c, NY * c + NY)
            fine[e, c] = dot2(hi[slot, rows], lo[slot, rows], table_ref[...])

    def out_copy(step):
        rows = pl.ds(2 * step, 2)
        return pltpu.make_async_copy(stage.at[:, rows], out_hbm.at[:, rows], sems.at[step])

    for e in range(3):
        make_fine(e)
    for step in range(8):
        if step < 7:
            make_fine(step + 3)
        for c in range(3):
            for h in range(2):
                cols = slice(128 * h, 128 * h + 128)
                for start in range(0, NY, 16):
                    rows = slice(start, start + 16)
                    lead = slice(LEAD + start, LEAD + start + 16)
                    centre = 3.0 * fine[step + 1, c, rows, cols]
                    low = g0_ref[c, 2 * step, h, lead] + (centre + fine[step, c, rows, cols])
                    high = g0_ref[c, 2 * step + 1, h, lead] + (centre + fine[step + 2, c, rows, cols])
                    stage[c, 2 * step, rows, cols] = low
                    stage[c, 2 * step + 1, rows, cols] = high
        out_copy(step).start()
    for step in range(8):
        out_copy(step).wait()


def final_call(sums, wide, table, g0):
    vmem = pl.BlockSpec(memory_space=pltpu.VMEM)
    return pl.pallas_call(
        final_kernel,
        out_shape=jax.ShapeDtypeStruct((3, ROWS, NY, NZ), F32),
        in_specs=[vmem] * 4,
        out_specs=pl.BlockSpec(memory_space=pltpu.HBM),
        scratch_shapes=[
            pltpu.VMEM((3, ROWS, NY, NZ), F32),
            pltpu.VMEM((2, 3 * NY, NZ), BF16),
            pltpu.VMEM((2, 3 * NY, NZ), BF16),
            pltpu.VMEM((10, 3, NY, NZ), F32),
            pltpu.SemaphoreType.DMA((8,)),
        ],
        compiler_params=pltpu.CompilerParams(vmem_limit_bytes=16 << 20),
        name="final_part",
    )(sums, wide, table, g0)


def shards(void_fraction, slip_velocity, size_class, class_scale):
    count = lax.axis_size("blk")
    even_pairs = [(i, i ^ 1) for i in range(count)]
    odd_pairs = [(i, (i + 1) % count if i % 2 else (i - 1) % count) for i in range(count)]
    void_fraction, slip_velocity, size_class = (
        pltpu.with_memory_space_constraint(x, pltpu.HBM) for x in (void_fraction, slip_velocity, size_class)
    )
    v_part, even_own, odd_own, fields, classes = linear_call(void_fraction, slip_velocity, size_class)
    odd_in = lax.ppermute(odd_own, "blk", odd_pairs)
    even_in = lax.ppermute(even_own, "blk", even_pairs)
    g0, filt, edge = drag_call(fields, classes, class_scale)
    wide, table, sums = levels_call(
        v_part, even_own, odd_own, even_in, odd_in, filt, edge, classes, class_scale
    )
    sums = lax.all_to_all(sums, "blk", 0, 0)
    return final_call(sums, wide, table, g0)


def solution(mesh):
    return jax.shard_map(
        shards,
        mesh=mesh,
        in_specs=(P("blk", None, "grp"), P(None, "blk", None, "grp"), P("blk", None, "grp"), P()),
        out_specs=P(None, "blk", None, "grp"),
        check_vma=False,
    )
```

time: 48.7 us -> 41 us (0.84)
  Pallas kernels: 22.9 us -> 16.9 us
  local copies, waits for them, and re-layouts: 5.1 us -> 0.01 us
  waiting for transfers between devices: 0.01 us -> 2.74 us
  blocking collectives: 13.2 us -> 13.9 us
    pallas_call x3, Pallas kernels: 17.1 us -> 11.3 us  [the longest x1 4.32 us: drag_call(): pl.pallas_call(drag_kernel, out_shape=(jax.ShapeDtypeStruct((3, ROWS, 2,...]
    unnamed x12 -> x2, local copies, waits for them, and re-layouts: 5.1 us -> 0.01 us
    ppermute x1, waiting for transfers between devices: 0.01 us -> 2.73 us  [shards(): odd_in = lax.ppermute(odd_own, 'blk', odd_pairs)]
    all_to_all x1, blocking collectives: 13.2 us -> 13.9 us  [shards(): sums = lax.all_to_all(sums, 'blk', 0, 0)]
  transfers between devices with their start and end apart: 2 -> 2, of which waited for: 0 -> 1; matrix products, arithmetic and copies ran while one was open for 0% -> 0% of each run, Pallas kernels for 16% -> 11%
where the time goes in v2:
time: 41 us; the launch traced here: 40.9 us
  Pallas kernels  16.9 us (41%)
  blocking collectives  13.9 us (34%)
  starting transfers between devices  7.25 us (18%)
  waiting for transfers between devices  2.74 us (7%)
    all_to_all x1, blocking collectives, shards(): sums = lax.all_to_all(sums, 'blk', 0, 0)  13.9 us
    pallas_call x1, Pallas kernels, linear_call(): pl.pallas_call(linear_kernel, out_shape=(jax.ShapeDtypeStruct((4, 8, 64,...  5.67 us
    ppermute x1, starting transfers between devices, shards(): odd_in = lax.ppermute(odd_own, 'blk', odd_pairs)  5.57 us
    pallas_call x1, Pallas kernels, drag_call(): pl.pallas_call(drag_kernel, out_shape=(jax.ShapeDtypeStruct((3, ROWS, 2,...  4.32 us
    pallas_call x1, Pallas kernels, final_call(): pl.pallas_call(final_kernel, out_shape=jax.ShapeDtypeStruct((3, ROWS, NY,...  3.81 us
    pallas_call x1, Pallas kernels, levels_call(): pl.pallas_call(levels_kernel, out_shape=(jax.ShapeDtypeStruct((60, NY, 12...  3.13 us
    ppermute x1, waiting for transfers between devices, shards(): odd_in = lax.ppermute(odd_own, 'blk', odd_pairs)  2.73 us
    ppermute x1, starting transfers between devices, shards(): even_in = lax.ppermute(even_own, 'blk', even_pairs)  1.68 us
  transfers between devices with their start and end apart: 2, of which 1 were waited for; matrix products, arithmetic and copies ran while one was open for 0% of the time, Pallas kernels for 11%

profile of v2, /device:TPU:0, one launch (start us, length us, event | category | flops | bytes accessed | tf_op | source)
XLA Modules:
  0.0 40.9 jit_solution(12812968826372049898)
XLA Ops:
  0.0 0.0 copy-start
  0.0 5.7 %linear_part.1 = (f32[4,8,64,128]{3,2,1,0:T(8,128)S(1)}, f32[608,128]{1,0:T(8,128)S(1)}, f32[608,128]{1,0:T(8,128)S(1)}, f32[4,16,2,144,128]{4,3,2,1,0:T(8,128)S(1)}, f32[2,16,32]{2,1,0:T(8,128)S(1)}) custom-call(f32[16,128,256]{2,1,0:T(8,128)} %void_hbm.1, f32[3,16,128,256]{3,2,1,0:T(8,128)} %slip_hbm.1, s32[2,16,32]{2,1,0:T(8,128)} %class_hbm.1), custom_call_target="tpu_custom_call" | custom-call | tf_op jit(solution)/shard_map/linear_part/pallas_call | solution.py:278
  5.7 1.7 %collective-permute-start = (f32[608,128]{1,0:T(8,128)S(1)}, f32[608,128]{1,0:T(8,128)S(1)}, u32[]{:S(2)}, u32[]{:S(2)}) collective-permute-start(f32[608,128]{1,0:T(8,128)S(1)} %get-tuple-element.17.even_own), channel_id=1, source_target_pairs={{0,1},{1,0},{2,3},{3,2},{4,5},{5,4},{6,7},{7,6},{8,9},{9,8},{10,11... | collective-permute-start | bytes 933896 | tf_op jit(solution)/shard_map/ppermute | solution.py:685
  7.4 5.6 %collective-permute-start.1 = (f32[608,128]{1,0:T(8,128)S(1)}, f32[608,128]{1,0:T(8,128)S(1)}, u32[]{:S(2)}, u32[]{:S(2)}) collective-permute-start(f32[608,128]{1,0:T(8,128)S(1)} %get-tuple-element.18.odd_own), channel_id=1, source_target_pairs={{0,15},{1,2},{2,1},{3,4},{4,3},{5,6},{6,5},{7,8},{8,7},{9,10},{10,... | collective-permute-start | bytes 933896 | tf_op jit(solution)/shard_map/ppermute | solution.py:684
  12.9 0.0 copy-done
  12.9 4.3 %drag_part.1 = (f32[3,16,2,144,128]{4,3,2,1,0:T(8,128)S(1)}, f32[3,8,64,128]{3,2,1,0:T(8,128)S(1)}, f32[2,3,64,128]{3,2,1,0:T(8,128)S(1)}) custom-call(f32[4,16,2,144,128]{4,3,2,1,0:T(8,128)S(1)} %get-tuple-element.19.fields, f32[2,16,32]{2,1,0:T(8,128)S(1)} %get-tuple-element.20.class_ref, f32[4]{0:T(128)S(1)} %copy-done), custom_call_target="tpu_custom_call" | custom-call | flops 60000000 | bytes 16000000 | tf_op jit(solution)/shard_map/drag_part/pallas_call | solution.py:373
  17.3 0.0 collective-permute-done.even_in
  17.3 2.7 %collective-permute-done.1.odd_in = f32[608,128]{1,0:T(8,128)S(1)} collective-permute-done((f32[608,128]{1,0:T(8,128)S(1)}, f32[608,128]{1,0:T(8,128)S(1)}, u32[]{:S(2)}, u32[]{:S(2)}) %collective-permute-start.1) | collective-permute-done | bytes 311328 | tf_op jit(solution)/shard_map/ppermute | solution.py:684
  20.0 3.1 %small_levels.1 = (f32[60,128,128]{2,1,0:T(8,128)S(1)}, bf16[256,256]{1,0:T(8,128)(2,1)S(1)}, f32[16,8,128]{2,1,0:T(8,128)S(1)}) custom-call(f32[4,8,64,128]{3,2,1,0:T(8,128)S(1)} %get-tuple-element.16.v_in, f32[608,128]{1,0:T(8,128)S(1)} %get-tuple-element.17.even_own, f32[608,128]{1,0:T(8,128)S(1)} %get-tuple-element.18.odd_own, ...), custom_call_target="tpu_custom_call" | custom-call | tf_op jit(solution)/shard_map/small_levels/pallas_call | solution.py:586
  23.1 13.9 %all_to_all.5.sums_ref = f32[16,8,128]{2,1,0:T(8,128)S(1)} all-to-all(f32[16,8,128]{2,1,0:T(8,128)S(1)} %get-tuple-element.23), channel_id=1, replica_groups=mesh['grp'=8,'blk'=16] {'blk'}, dimensions={0} | all-to-all | bytes 131072 | tf_op jit(solution)/shard_map/all_to_all | solution.py:690
  37.0 3.8 %final_part.1 = f32[3,16,128,256]{3,2,1,0:T(8,128)} custom-call(f32[16,8,128]{2,1,0:T(8,128)S(1)} %all_to_all.5.sums_ref, f32[60,128,128]{2,1,0:T(8,128)S(1)} %get-tuple-element.24.wide_ref, bf16[256,256]{1,0:T(8,128)(2,1)S(1)} %get-tuple-element.25.table_ref, f32[3,16,2,144,128]{4,3,2,1,0:T(8,128)S(1)} %get-tuple-element.26.g0_ref), custom_call_target="tpu_custom_call" | custom-call | tf_op jit(solution)/shard_map/final_part/pallas_call | solution.py:659
Async XLA Ops:
  0.0 12.9 %copy-start = (f32[4]{0:T(128)S(1)}, f32[4]{0:T(128)}, u32[]{:S(2)}) copy-start(f32[4]{0:T(128)} %scale_ref.3) | copy-start | bytes 52
  5.7 11.6 %collective-permute-start = (f32[608,128]{1,0:T(8,128)S(1)}, f32[608,128]{1,0:T(8,128)S(1)}, u32[]{:S(2)}, u32[]{:S(2)}) collective-permute-start(f32[608,128]{1,0:T(8,128)S(1)} %get-tuple-element.17.even_own), channel_id=1, source_target_pairs={{0,1},{1,0},{2,3},{3,2},{4,5},{5,4},{6,7},{7,6},{8,9},{9,8},{10,11... | collective-permute-start | bytes 933896 | tf_op jit(solution)/shard_map/ppermute | solution.py:685
  7.4 12.6 %collective-permute-start.1 = (f32[608,128]{1,0:T(8,128)S(1)}, f32[608,128]{1,0:T(8,128)S(1)}, u32[]{:S(2)}, u32[]{:S(2)}) collective-permute-start(f32[608,128]{1,0:T(8,128)S(1)} %get-tuple-element.18.odd_own), channel_id=1, source_target_pairs={{0,15},{1,2},{2,1},{3,4},{4,3},{5,6},{6,5},{7,8},{8,7},{9,10},{10,... | collective-permute-start | bytes 933896 | tf_op jit(solution)/shard_map/ppermute | solution.py:684

commit v3 on v2

--- a/solution.py
+++ b/solution.py
@@ -6,6 +6,7 @@
 from jax.experimental import pallas as pl
 from jax.experimental.pallas import tpu as pltpu
 from jax.sharding import PartitionSpec as P
+
 
 F32 = jnp.float32
 BF16 = jnp.bfloat16
@@ -144,7 +145,6 @@
 
 def linear_kernel(void_hbm, slip_hbm, class_hbm, v_ref, even_ref, odd_ref, fields, class_ref, ybuf, hi, lo, wbuf, pad2, pad3, classes, sems, class_sem):
     parity = lax.axis_index("blk") % 2
-    pairs = ROWS // 2
 
     def copies(k):
         rows = pl.ds(2 * k, 2)
@@ -158,7 +158,8 @@
 
     class_copy = pltpu.make_async_copy(class_hbm, classes, class_sem)
     class_copy.start()
-    for k in range(pairs):
+    order = (0, 7, 1, 6, 2, 5, 3, 4)
+    for k in order:
         for copy in copies(k):
             copy.start()
     for c in range(4):
@@ -194,16 +195,6 @@
         for c in range(4):
             v_ref[c, i] = out[c * 64 : c * 64 + 64]
 
-    along_y(0)
-
-    def body(i, carry):
-        along_y(i + 1)
-        along_x(i, 0)
-        return carry
-
-    lax.fori_loop(0, pairs - 1, body, 0)
-    along_x(pairs - 1, 0)
-
     def side_rows(ref, last, at):
         r0 = jnp.where(last == 1, ROWS, 1)
         r1 = jnp.where(last == 1, ROWS - 1, 2)
@@ -213,8 +204,16 @@
             x_rows(ybuf, c, (r0, r1, r2), (3, 3, 1), hi, lo, at + 256 + 64 * c)
         ref[0:512] = dot2(hi[at : at + 512], lo[at : at + 512], table)
 
-    side_rows(even_ref, 1 - parity, 256)
-    side_rows(odd_ref, parity, 768)
+    for k in order[:4]:
+        along_y(k)
+    along_x(0, 0)
+    along_x(7, 256 * 7)
+    side_rows(even_ref, 1 - parity, 2048)
+    side_rows(odd_ref, parity, 2560)
+    for k, ready in zip(order[4:], ((1,), (6,), (2,), (3, 4, 5))):
+        along_y(k)
+        for i in ready:
+            along_x(i, 256 * i)
 
     table2 = restrict_z(128)
     for m in range(2):
@@ -288,8 +287,8 @@
         out_specs=(vmem,) * 5,
         scratch_shapes=[
             pltpu.VMEM((4, ROWS + 2, 2, 64, 128), F32),
-            pltpu.VMEM((1280, NZ), BF16),
-            pltpu.VMEM((1280, NZ), BF16),
+            pltpu.VMEM((3072, NZ), BF16),
+            pltpu.VMEM((3072, NZ), BF16),
             pltpu.VMEM((4, 2, 32, 64), F32),
             pltpu.VMEM((16, 64 + 16, 128), F32),
             pltpu.VMEM((8, 32 + 16, 128), F32),
@@ -297,7 +296,7 @@
             pltpu.SemaphoreType.DMA((8, 4)),
             pltpu.SemaphoreType.DMA,
         ],
-        compiler_params=pltpu.CompilerParams(vmem_limit_bytes=12 << 20),
+        compiler_params=pltpu.CompilerParams(vmem_limit_bytes=14 << 20),
         name="linear_part",
     )(void, slip, classes)
 
@@ -406,7 +405,7 @@
     return (jnp.where(coarse == centre, 3.0, 0.0) + jnp.where(coarse == neighbour, 1.0, 0.0)).astype(BF16)
 
 
-def prolong_levels(g1_ref, g2_ref, g3_ref, wide_ref, table_ref, pad3, up3, pad2, up2, pad1):
+def make_table(table_ref):
     first = plain_prolong_z(128)
     second = jnp.dot(plain_prolong_z(64), first, preferred_element_type=F32)
     third = jnp.dot(plain_prolong_z(32), plain_prolong_z(64), preferred_element_type=F32)
@@ -415,34 +414,110 @@
     table_ref[128:192] = (second * (1.0 / 64.0**2)).astype(BF16)
     table_ref[192:224] = (third * (1.0 / 64.0**3)).astype(BF16)
     table_ref[224:256] = jnp.zeros((32, NZ), BF16)
-    for c in range(3):
-        for e in range(4):
-            p = 4 * c + e
-            pad3[p, LEAD : LEAD + 16, 0:32] = g3_ref[c, e]
-            wrap_rows(pad3, p, 16)
-            prolong_y(pad3, p, 16, up3, p)
-        for f, value in x_prolong(lambda e: up3[4 * c + e], 2):
-            both = jnp.concatenate([g2_ref[c, f], value[:, 0:32], jnp.zeros((32, 32), F32)], axis=1)
-            p = 6 * c + f
-            pad2[p, LEAD : LEAD + 32] = both
-            wrap_rows(pad2, p, 32)
-            prolong_y(pad2, p, 32, up2, p)
-        for f, value in x_prolong(lambda e: up2[6 * c + e], 4):
-            p = 10 * c + f
-            for h, part in enumerate((g1_ref[c, f], value)):
-                q = 2 * p + h
-                pad1[q, LEAD : LEAD + 64] = part
-                wrap_rows(pad1, q, 64)
-                prolong_y(pad1, q, 64, wide_ref, q)
+
+
+def put_wide(pad, q, part, wide, to):
+    pad[q, LEAD : LEAD + 64] = part
+    wrap_rows(pad, q, 64)
+    prolong_y(pad, q, 64, wide, to)
+
+
+def x_part(plane, c, i, count):
+    def part(start, step):
+        rows = pl.ds(start, step)
+        if i == -1:
+            return 3.0 * plane(c, -1)[rows] + plane(c, 0)[rows]
+        if i == count:
+            return plane(c, 2 * count - 1)[rows] + 3.0 * plane(c, 2 * count)[rows]
+        return (plane(c, 2 * i - 1)[rows] + plane(c, 2 * i + 2)[rows]) + 3.0 * (
+            plane(c, 2 * i)[rows] + plane(c, 2 * i + 1)[rows]
+        )
+
+    return part
+
+
+def total(values):
+    return jnp.sum(values, axis=0, keepdims=True)
+
+
+def inner_kernel(v_in, filt_ref, class_ref, scale_ref, g1_ref, w_ref, g2_ref, wide_ref, table_ref, kap1_ref, kap2_ref, sums_ref, pad, pad1, hi, lo):
+    make_table(table_ref)
+    for b in range(2):
+        kap1_ref[b] = class_factor(scale_ref, spread(class_ref[b], 64, 128))
+        kap2_ref[b] = class_factor(scale_ref, spread(class_ref[b], 32, 64))
+    numerator = jnp.zeros((64, 128), F32)
+    denominator = jnp.zeros((64, 128), F32)
+    for i in range(1, 7):
+        slips = v_in[1, i], v_in[2, i], v_in[3, i]
+        g = drag(v_in[0, i], *slips, kap1_ref[i // 4])
+        for c in range(3):
+            g1_ref[c, i - 1] = g[c]
+            numerator += filt_ref[c, i] * slips[c]
+            denominator += g[c] * slips[c]
+            put_wide(pad1, 6 * c + i - 1, g[c], wide_ref, 6 * c + i - 1)
+    sums_ref[0:1] = total(numerator)
+    sums_ref[1:2] = total(denominator)
+    n = 0
+    for count, plane in ((4, lambda c, i: v_in.at[c, i]), (3, lambda c, i: g1_ref.at[c, i - 1])):
+        for i in (1, 2):
+            for c in range(count):
+                fill_pad(pad, n, x_part(plane, c, i, 4), 64, 32, 128)
+                restrict_y(pad, n, 64, hi, lo, 32 * n, 128)
+                n += 1
+    out = dot2(hi[...], lo[...], restrict_z(128))
+    numerator = jnp.zeros((32, 64), F32)
+    denominator = jnp.zeros((32, 64), F32)
+    for i in (1, 2):
+        channels = [out[32 * (4 * (i - 1) + c) : 32 * (4 * (i - 1) + c) + 32] for c in range(4)]
+        g = drag(*channels, kap2_ref[i // 2])
+        for c in range(4):
+            w_ref[c, i - 1] = channels[c]
+        for c in range(3):
+            g2_ref[c, i - 1] = g[c]
+            at = 32 * (8 + 3 * (i - 1) + c)
+            numerator += out[at : at + 32] * channels[c + 1]
+            denominator += g[c] * channels[c + 1]
+    blank = jnp.zeros((1, 64), F32)
+    sums_ref[2:3] = jnp.concatenate([total(numerator), blank], axis=1)
+    sums_ref[3:4] = jnp.concatenate([total(denominator), blank], axis=1)
+    sums_ref[4:8] = jnp.zeros((4, 128), F32)
+
+
+def inner_call(v_part, filt, classes, scale):
+    vmem = pl.BlockSpec(memory_space=pltpu.VMEM)
+    return pl.pallas_call(
+        inner_kernel,
+        out_shape=(
+            jax.ShapeDtypeStruct((3, 6, 64, 128), F32),
+            jax.ShapeDtypeStruct((4, 2, 32, 64), F32),
+            jax.ShapeDtypeStruct((3, 2, 32, 64), F32),
+            jax.ShapeDtypeStruct((18, NY, 128), F32),
+            jax.ShapeDtypeStruct((256, NZ), BF16),
+            jax.ShapeDtypeStruct((2, 64, 128), F32),
+            jax.ShapeDtypeStruct((2, 32, 64), F32),
+            jax.ShapeDtypeStruct((8, 128), F32),
+        ),
+        in_specs=[vmem] * 3 + [pl.BlockSpec(memory_space=pltpu.SMEM)],
+        out_specs=(vmem,) * 8,
+        scratch_shapes=[
+            pltpu.VMEM((14, 64 + 16, 128), F32),
+            pltpu.VMEM((18, 64 + 16, 128), F32),
+            pltpu.VMEM((14 * 32, 128), BF16),
+            pltpu.VMEM((14 * 32, 128), BF16),
+        ],
+        compiler_params=pltpu.CompilerParams(vmem_limit_bytes=8 << 20),
+        cost_estimate=pl.CostEstimate(flops=20_000_000, bytes_accessed=4_000_000, transcendentals=300_000),
+        name="inner_levels",
+    )(v_part, filt, classes, scale)
 
 
 def levels_kernel(
     v_in, even_own, odd_own, even_in, odd_in, filt_ref, edge_ref, class_ref, scale_ref,
-    wide_ref, table_ref, sums_ref,
-    v, w, g1_ref, g2_ref, g3_ref, gpad, pad, hi, lo, kap, pad3, up3, pad2, up2, pad1,
+    g1_in, w_in, g2_in, kap1_ref, kap2_ref, part_ref,
+    wide_ref, sums_ref,
+    v, g1, w, g2, g3, pad, padw, hi, lo, pad3, up3, pad2, up2, pad1,
 ):
-    parity = lax.axis_index("blk") % 2
-    is_even = parity == 0
+    is_even = lax.axis_index("blk") % 2 == 0
 
     def left(rows):
         return jnp.where(is_even, odd_in[rows], even_in[rows])
@@ -455,175 +530,191 @@
 
     def own_last(rows):
         return jnp.where(is_even, even_own[rows], odd_own[rows])
+
+    slot1 = {-1: 0, 0: 1, 7: 2, 8: 3}
+    slot2 = {-1: 0, 0: 1, 3: 2, 4: 3}
+
+    def plane_v(c, i):
+        return v.at[c, slot1[i]] if i in slot1 else v_in.at[c, i]
+
+    def plane_g1(c, i):
+        return g1.at[c, slot1[i]] if i in slot1 else g1_in.at[c, i - 1]
+
+    def plane_w(c, i):
+        return w.at[c, slot2[i]] if i in slot2 else w_in.at[c, i - 1]
+
+    def plane_g2(c, i):
+        return g2.at[c, slot2[i]] if i in slot2 else g2_in.at[c, i - 1]
 
     for c in range(4):
         outer = slice(64 * c, 64 * c + 64)
         combined = slice(256 + 64 * c, 256 + 64 * c + 64)
         v[c, 0] = left(combined) + own_first(outer)
         v[c, 1] = v_in[c, 0] + left(outer)
-        for i in range(1, 7):
-            v[c, i + 1] = v_in[c, i]
-        v[c, 8] = v_in[c, 7] + right(outer)
-        v[c, 9] = right(combined) + own_last(outer)
-    blocks = [
-        left(slice(592, 608))[:, 0:32],
-        class_ref[0],
-        class_ref[1],
-        right(slice(592, 608))[:, 0:32],
-    ]
-    for b in range(4):
-        kap[b] = class_factor(scale_ref, spread(blocks[b], 64, 128))
+        v[c, 2] = v_in[c, 7] + right(outer)
+        v[c, 3] = right(combined) + own_last(outer)
+    beyond = left(slice(592, 608))[:, 0:32], right(slice(592, 608))[:, 0:32]
+    factors = {
+        -1: class_factor(scale_ref, spread(beyond[0], 64, 128)),
+        0: kap1_ref[0],
+        7: kap1_ref[1],
+        8: class_factor(scale_ref, spread(beyond[1], 64, 128)),
+    }
     numerator = jnp.zeros((64, 128), F32)
     denominator = jnp.zeros((64, 128), F32)
-    for i in range(10):
-        slips = v[1, i], v[2, i], v[3, i]
-        g = drag(v[0, i], *slips, kap[(i + 3) // 4])
-        for c in range(3):
-            g1_ref[c, i] = g[c]
-            if i == 0:
+    for i, n in slot1.items():
+        slips = v[1, n], v[2, n], v[3, n]
+        g = drag(v[0, n], *slips, factors[i])
+        for c in range(3):
+            g1[c, n] = g[c]
+            if i == -1:
                 numerator += edge_ref[0, c] * slips[c]
-            elif i == 9:
+            elif i == 8:
                 numerator += edge_ref[1, c] * slips[c]
             else:
-                numerator += filt_ref[c, i - 1] * slips[c]
+                numerator += filt_ref[c, i] * slips[c]
                 denominator += g[c] * slips[c]
-    sums = [jnp.sum(numerator, axis=0, keepdims=True), jnp.sum(denominator, axis=0, keepdims=True)]
-
-    table2 = restrict_z(128)
-
-    def x_part(src, c, i, count):
-        def part(start, step):
-            rows = pl.ds(start, step)
-            if i == -1:
-                return 3.0 * src[c, 0, rows] + src[c, 1, rows]
-            if i == count:
-                return src[c, 2 * count, rows] + 3.0 * src[c, 2 * count + 1, rows]
-            return (src[c, 2 * i, rows] + src[c, 2 * i + 3, rows]) + 3.0 * (
-                src[c, 2 * i + 1, rows] + src[c, 2 * i + 2, rows]
-            )
-
-        return part
+    sums = [total(numerator) + part_ref[0:1], total(denominator) + part_ref[1:2]]
 
     n = 0
-    for i in range(-1, 5):
-        for c in range(4):
-            fill_pad(pad, n, x_part(v, c, i, 4), 64, 32, 128)
-            restrict_y(pad, n, 64, hi, lo, 32 * n, 128)
-            n += 1
-    for i in range(4):
-        for c in range(3):
-            fill_pad(pad, n, x_part(g1_ref, c, i, 4), 64, 32, 128)
-            restrict_y(pad, n, 64, hi, lo, 32 * n, 128)
-            n += 1
-    out = dot2(hi[0 : 32 * n, 0:128], lo[0 : 32 * n, 0:128], table2)
-    for i in range(6):
-        for c in range(4):
-            value = out[32 * (4 * i + c) : 32 * (4 * i + c) + 32]
-            if i == 0 or i == 5:
-                rows = slice(512 + 32 * (c // 2), 544 + 32 * (c // 2))
-                beyond = left(rows) if i == 0 else right(rows)
-                if c % 2:
-                    beyond = pltpu.roll(beyond, 64, 1)
-                value = value + beyond[:, 0:64]
-            w[c, i] = value
+    for count, plane, rows in ((4, plane_v, (-1, 0, 3, 4)), (3, plane_g1, (0, 3))):
+        for i in rows:
+            for c in range(count):
+                fill_pad(pad, n, x_part(plane, c, i, 4), 64, 32, 128)
+                restrict_y(pad, n, 64, hi, lo, 32 * n, 128)
+                n += 1
+    out = dot2(hi[0 : 32 * n, 0:128], lo[0 : 32 * n, 0:128], restrict_z(128))
+    factors = {
+        -1: class_factor(scale_ref, spread(beyond[0], 32, 64)),
+        0: kap2_ref[0],
+        3: kap2_ref[1],
+        4: class_factor(scale_ref, spread(beyond[1], 32, 64)),
+    }
     numerator = jnp.zeros((32, 64), F32)
     denominator = jnp.zeros((32, 64), F32)
-    factors = [class_factor(scale_ref, spread(block, 32, 64)) for block in blocks]
-    for i in range(6):
-        slips = w[1, i], w[2, i], w[3, i]
-        g = drag(w[0, i], *slips, factors[(i + 1) // 2])
-        for c in range(3):
-            g2_ref[c, i] = g[c]
-            if 1 <= i <= 4:
-                at = 32 * (24 + 3 * (i - 1) + c)
-                numerator += out[at : at + 32] * slips[c]
-                denominator += g[c] * slips[c]
-    sums += [jnp.sum(numerator, axis=0, keepdims=True), jnp.sum(denominator, axis=0, keepdims=True)]
-
-    table3 = restrict_z(64)
+    for i, n in slot2.items():
+        channels = []
+        for c in range(4):
+            value = out[32 * (4 * n + c) : 32 * (4 * n + c) + 32]
+            if i in (-1, 4):
+                rows = slice(512 + 32 * (c // 2), 544 + 32 * (c // 2))
+                more = left(rows) if i == -1 else right(rows)
+                if c % 2:
+                    more = pltpu.roll(more, 64, 1)
+                value = value + more[:, 0:64]
+            w[c, n] = value
+            channels.append(value)
+        g = drag(*channels, factors[i])
+        for c in range(3):
+            g2[c, n] = g[c]
+            if i in (0, 3):
+                at = 32 * (16 + 3 * (n - 1) + c)
+                numerator += out[at : at + 32] * channels[c + 1]
+                denominator += g[c] * channels[c + 1]
+    sums += [total(numerator) + part_ref[2:3, 0:64], total(denominator) + part_ref[3:4, 0:64]]
+
     n = 0
-    for i in range(-1, 3):
-        for c in range(4):
-            fill_pad(gpad, n, x_part(w, c, i, 2), 32, 32, 64)
-            restrict_y(gpad, n, 32, hi, lo, 16 * n, 64)
-            n += 1
-    for i in range(2):
-        for c in range(3):
-            fill_pad(gpad, n, x_part(g2_ref, c, i, 2), 32, 32, 64)
-            restrict_y(gpad, n, 32, hi, lo, 16 * n, 64)
-            n += 1
-    out = dot2(hi[0 : 16 * n, 0:64], lo[0 : 16 * n, 0:64], table3)
+    for count, plane, rows in ((4, plane_w, (-1, 0, 1, 2)), (3, plane_g2, (0, 1))):
+        for i in rows:
+            for c in range(count):
+                fill_pad(padw, n, x_part(plane, c, i, 2), 32, 32, 64)
+                restrict_y(padw, n, 32, hi, lo, 16 * n, 64)
+                n += 1
+    out = dot2(hi[0 : 16 * n, 0:64], lo[0 : 16 * n, 0:64], restrict_z(64))
     numerator = jnp.zeros((16, 32), F32)
     denominator = jnp.zeros((16, 32), F32)
+    blocks = [beyond[0], class_ref[0], class_ref[1], beyond[1]]
     for i in range(4):
         channels = []
         for c in range(4):
             value = out[16 * (4 * i + c) : 16 * (4 * i + c) + 16]
             if i == 0 or i == 3:
-                beyond = left(slice(576, 592)) if i == 0 else right(slice(576, 592))
+                more = left(slice(576, 592)) if i == 0 else right(slice(576, 592))
                 if c:
-                    beyond = pltpu.roll(beyond, 128 - 32 * c, 1)
-                value = value + beyond[:, 0:32]
+                    more = pltpu.roll(more, 128 - 32 * c, 1)
+                value = value + more[:, 0:32]
             channels.append(value)
         g = drag(*channels, class_factor(scale_ref, blocks[i]))
         for c in range(3):
-            g3_ref[c, i] = g[c]
+            g3[c, i] = g[c]
             if 1 <= i <= 2:
                 at = 16 * (16 + 3 * (i - 1) + c)
                 numerator += out[at : at + 16] * channels[c + 1]
                 denominator += g[c] * channels[c + 1]
-    sums += [jnp.sum(numerator, axis=0, keepdims=True), jnp.sum(denominator, axis=0, keepdims=True)]
+    sums += [total(numerator), total(denominator)]
     ones = jnp.ones((1, 32), F32)
     packed = [sums[0], sums[1]] + [jnp.concatenate([sums[2 + k], sums[4 + k], ones], axis=1) for k in range(2)]
     tile = jnp.concatenate(packed + [jnp.zeros((4, 128), F32)], axis=0)
     for d in range(16):
         sums_ref[d] = tile
-    prolong_levels(g1_ref, g2_ref, g3_ref, wide_ref, table_ref, pad3, up3, pad2, up2, pad1)
-
-
-def levels_call(v_part, even_own, odd_own, even_in, odd_in, filt, edge, classes, scale):
+
+    for c in range(3):
+        for e in range(4):
+            p = 4 * c + e
+            pad3[p, LEAD : LEAD + 16, 0:32] = g3[c, e]
+            wrap_rows(pad3, p, 16)
+            prolong_y(pad3, p, 16, up3, p)
+        for f, value in x_prolong(lambda e: up3[4 * c + e], 2):
+            p = 6 * c + f
+            pad2[p, LEAD : LEAD + 32] = jnp.concatenate(
+                [plane_g2(c, f - 1)[...], value[:, 0:32], jnp.zeros((32, 32), F32)], axis=1
+            )
+            wrap_rows(pad2, p, 32)
+            prolong_y(pad2, p, 32, up2, p)
+        for f, value in x_prolong(lambda e: up2[6 * c + e], 4):
+            put_wide(pad1, 10 * c + f, value, wide_ref, 10 * c + f)
+        for n in slot1.values():
+            put_wide(pad1, 30 + 4 * c + n, g1[c, n], wide_ref, 30 + 4 * c + n)
+
+
+def levels_call(v_part, even_own, odd_own, even_in, odd_in, filt, edge, classes, scale, g1, w, g2, kap1, kap2, part):
     vmem = pl.BlockSpec(memory_space=pltpu.VMEM)
     return pl.pallas_call(
         levels_kernel,
         out_shape=(
-            jax.ShapeDtypeStruct((60, NY, 128), F32),
-            jax.ShapeDtypeStruct((256, NZ), BF16),
+            jax.ShapeDtypeStruct((42, NY, 128), F32),
             jax.ShapeDtypeStruct((16, 8, 128), F32),
         ),
-        in_specs=[vmem] * 8 + [pl.BlockSpec(memory_space=pltpu.SMEM)],
-        out_specs=(vmem,) * 3,
+        in_specs=[vmem] * 8 + [pl.BlockSpec(memory_space=pltpu.SMEM)] + [vmem] * 6,
+        out_specs=(vmem,) * 2,
         scratch_shapes=[
-            pltpu.VMEM((4, 10, 64, 128), F32),
-            pltpu.VMEM((4, 6, 32, 64), F32),
-            pltpu.VMEM((3, 10, 64, 128), F32),
-            pltpu.VMEM((3, 6, 32, 64), F32),
+            pltpu.VMEM((4, 4, 64, 128), F32),
+            pltpu.VMEM((3, 4, 64, 128), F32),
+            pltpu.VMEM((4, 4, 32, 64), F32),
+            pltpu.VMEM((3, 4, 32, 64), F32),
             pltpu.VMEM((3, 4, 16, 32), F32),
+            pltpu.VMEM((22, 64 + 16, 128), F32),
             pltpu.VMEM((22, 32 + 16, 128), F32),
-            pltpu.VMEM((36, 64 + 16, 128), F32),
-            pltpu.VMEM((36 * 32, 128), BF16),
-            pltpu.VMEM((36 * 32, 128), BF16),
-            pltpu.VMEM((4, 64, 128), F32),
+            pltpu.VMEM((22 * 32, 128), BF16),
+            pltpu.VMEM((22 * 32, 128), BF16),
             pltpu.VMEM((12, 16 + 16, 128), F32),
             pltpu.VMEM((12, 32, 128), F32),
             pltpu.VMEM((18, 32 + 16, 128), F32),
             pltpu.VMEM((18, 64, 128), F32),
-            pltpu.VMEM((60, 64 + 16, 128), F32),
+            pltpu.VMEM((42, 64 + 16, 128), F32),
         ],
-        compiler_params=pltpu.CompilerParams(vmem_limit_bytes=14 << 20),
+        compiler_params=pltpu.CompilerParams(vmem_limit_bytes=12 << 20),
         name="small_levels",
-    )(v_part, even_own, odd_own, even_in, odd_in, filt, edge, classes, scale)
-
-
-def final_kernel(sums_ref, wide_ref, table_ref, g0_ref, out_hbm, stage, hi, lo, fine, sems):
-    total = jnp.sum(sums_ref[...], axis=0)
-    ratios = [total[2 * h : 2 * h + 1] / total[2 * h + 1 : 2 * h + 2] - 1.0 for h in range(2)]
+    )(v_part, even_own, odd_own, even_in, odd_in, filt, edge, classes, scale, g1, w, g2, kap1, kap2, part)
+
+
+def final_kernel(sums_ref, inner_ref, wide_ref, table_ref, g0_ref, out_hbm, stage, hi, lo, fine, sems):
+    added = jnp.sum(sums_ref[...], axis=0)
+    ratios = [added[2 * h : 2 * h + 1] / added[2 * h + 1 : 2 * h + 2] - 1.0 for h in range(2)]
+
+    def wide(c, e, h):
+        if h:
+            return wide_ref.at[10 * c + e]
+        if 2 <= e <= 7:
+            return inner_ref.at[6 * c + e - 2]
+        return wide_ref.at[30 + 4 * c + {0: 0, 1: 1, 8: 2, 9: 3}[e]]
 
     def make_fine(e):
         slot = e % 2
         for c in range(3):
             for h in range(2):
                 for start in range(0, NY, 16):
-                    value = wide_ref[20 * c + 2 * e + h, start : start + 16] * ratios[h]
+                    value = wide(c, e, h)[start : start + 16] * ratios[h]
                     split_at(value, hi.at[slot], lo.at[slot], NY * c + start, 128 * h)
         for c in range(3):
             rows = slice(NY * c, NY * c + NY)
@@ -654,12 +745,12 @@
         out_copy(step).wait()
 
 
-def final_call(sums, wide, table, g0):
+def final_call(sums, inner, wide, table, g0):
     vmem = pl.BlockSpec(memory_space=pltpu.VMEM)
     return pl.pallas_call(
         final_kernel,
         out_shape=jax.ShapeDtypeStruct((3, ROWS, NY, NZ), F32),
-        in_specs=[vmem] * 4,
+        in_specs=[vmem] * 5,
         out_specs=pl.BlockSpec(memory_space=pltpu.HBM),
         scratch_shapes=[
             pltpu.VMEM((3, ROWS, NY, NZ), F32),
@@ -670,7 +761,7 @@
         ],
         compiler_params=pltpu.CompilerParams(vmem_limit_bytes=16 << 20),
         name="final_part",
-    )(sums, wide, table, g0)
+    )(sums, inner, wide, table, g0)
 
 
 def shards(void_fraction, slip_velocity, size_class, class_scale):
@@ -684,11 +775,12 @@
     odd_in = lax.ppermute(odd_own, "blk", odd_pairs)
     even_in = lax.ppermute(even_own, "blk", even_pairs)
     g0, filt, edge = drag_call(fields, classes, class_scale)
-    wide, table, sums = levels_call(
-        v_part, even_own, odd_own, even_in, odd_in, filt, edge, classes, class_scale
+    g1, w, g2, inner, table, kap1, kap2, part = inner_call(v_part, filt, classes, class_scale)
+    wide, sums = levels_call(
+        v_part, even_own, odd_own, even_in, odd_in, filt, edge, classes, class_scale, g1, w, g2, kap1, kap2, part
     )
     sums = lax.all_to_all(sums, "blk", 0, 0)
-    return final_call(sums, wide, table, g0)
+    return final_call(sums, inner, wide, table, g0)
 
 
 def solution(mesh):

time: 41 us -> 40.3 us (0.983)
  waiting for transfers between devices: 2.74 us -> 1.17 us
  Pallas kernels: 16.9 us -> 17.8 us
    ppermute x1, waiting for transfers between devices: 2.73 us -> 1.17 us  [shards(): odd_in = lax.ppermute(odd_own, 'blk', odd_pairs)]
    pallas_call x1 -> x2, Pallas kernels: 3.13 us -> 3.81 us  [the longest x1 2.25 us: levels_call(): pl.pallas_call(levels_kernel, out_shape=(jax.ShapeDtypeStruct((42, NY, 12...]
  transfers between devices with their start and end apart: 2 -> 2, of which waited for: 1 -> 1; matrix products, arithmetic and copies ran while one was open for 0% -> 0% of each run, Pallas kernels for 11% -> 15%
where the time goes in v3:
time: 40.3 us; the launch traced here: 40.1 us
  Pallas kernels  17.8 us (44%)
  blocking collectives  13.9 us (34%)
  starting transfers between devices  7.25 us (18%)
  waiting for transfers between devices  1.17 us (3%)
    all_to_all x1, blocking collectives, shards(): sums = lax.all_to_all(sums, 'blk', 0, 0)  13.9 us
    pallas_call x1, Pallas kernels, linear_call(): pl.pallas_call(linear_kernel, out_shape=(jax.ShapeDtypeStruct((4, 8, 64,...  5.74 us
    ppermute x1, starting transfers between devices, shards(): odd_in = lax.ppermute(odd_own, 'blk', odd_pairs)  5.57 us
    pallas_call x1, Pallas kernels, drag_call(): pl.pallas_call(drag_kernel, out_shape=(jax.ShapeDtypeStruct((3, ROWS, 2,...  4.32 us
    pallas_call x1, Pallas kernels, final_call(): pl.pallas_call(final_kernel, out_shape=jax.ShapeDtypeStruct((3, ROWS, NY,...  3.89 us
    pallas_call x1, Pallas kernels, levels_call(): pl.pallas_call(levels_kernel, out_shape=(jax.ShapeDtypeStruct((42, NY, 12...  2.25 us
    ppermute x1, starting transfers between devices, shards(): even_in = lax.ppermute(even_own, 'blk', even_pairs)  1.68 us
    pallas_call x1, Pallas kernels, inner_call(): pl.pallas_call(inner_kernel, out_shape=(jax.ShapeDtypeStruct((3, 6, 64, 1...  1.56 us
  transfers between devices with their start and end apart: 2, of which 1 were waited for; matrix products, arithmetic and copies ran while one was open for 0% of the time, Pallas kernels for 15%

profile of v3, /device:TPU:0, one launch (start us, length us, event | category | flops | bytes accessed | tf_op | source)
XLA Modules:
  0.0 40.1 jit_solution(14973649135381556458)
XLA Ops:
  0.0 0.0 copy-start
  0.0 5.7 %linear_part.1 = (f32[4,8,64,128]{3,2,1,0:T(8,128)S(1)}, f32[608,128]{1,0:T(8,128)S(1)}, f32[608,128]{1,0:T(8,128)S(1)}, f32[4,16,2,144,128]{4,3,2,1,0:T(8,128)S(1)}, f32[2,16,32]{2,1,0:T(8,128)S(1)}) custom-call(f32[16,128,256]{2,1,0:T(8,128)} %void_hbm.1, f32[3,16,128,256]{3,2,1,0:T(8,128)} %slip_hbm.1, s32[2,16,32]{2,1,0:T(8,128)} %class_hbm.1), custom_call_target="tpu_custom_call" | custom-call | tf_op jit(solution)/shard_map/linear_part/pallas_call | solution.py:277
  5.7 1.7 %collective-permute-start = (f32[608,128]{1,0:T(8,128)S(1)}, f32[608,128]{1,0:T(8,128)S(1)}, u32[]{:S(2)}, u32[]{:S(2)}) collective-permute-start(f32[608,128]{1,0:T(8,128)S(1)} %get-tuple-element.24.even_own), channel_id=1, source_target_pairs={{0,1},{1,0},{2,3},{3,2},{4,5},{5,4},{6,7},{7,6},{8,9},{9,8},{10,11... | collective-permute-start | bytes 933896 | tf_op jit(solution)/shard_map/ppermute | solution.py:776
  7.4 5.6 %collective-permute-start.1 = (f32[608,128]{1,0:T(8,128)S(1)}, f32[608,128]{1,0:T(8,128)S(1)}, u32[]{:S(2)}, u32[]{:S(2)}) collective-permute-start(f32[608,128]{1,0:T(8,128)S(1)} %get-tuple-element.25.odd_own), channel_id=1, source_target_pairs={{0,15},{1,2},{2,1},{3,4},{4,3},{5,6},{6,5},{7,8},{8,7},{9,10},{10,... | collective-permute-start | bytes 933896 | tf_op jit(solution)/shard_map/ppermute | solution.py:775
  13.0 0.0 copy-done
  13.0 4.3 %drag_part.1 = (f32[3,16,2,144,128]{4,3,2,1,0:T(8,128)S(1)}, f32[3,8,64,128]{3,2,1,0:T(8,128)S(1)}, f32[2,3,64,128]{3,2,1,0:T(8,128)S(1)}) custom-call(f32[4,16,2,144,128]{4,3,2,1,0:T(8,128)S(1)} %get-tuple-element.26.fields, f32[2,16,32]{2,1,0:T(8,128)S(1)} %get-tuple-element.27.class_ref, f32[4]{0:T(128)S(1)} %copy-done), custom_call_target="tpu_custom_call" | custom-call | flops 60000000 | bytes 16000000 | tf_op jit(solution)/shard_map/drag_part/pallas_call | solution.py:372
  17.3 1.6 %inner_levels.1 = (f32[3,6,64,128]{3,2,1,0:T(8,128)S(1)}, f32[4,2,32,64]{3,2,1,0:T(8,128)S(1)}, f32[3,2,32,64]{3,2,1,0:T(8,128)S(1)}, f32[18,128,128]{2,1,0:T(8,...) custom-call(f32[4,8,64,128]{3,2,1,0:T(8,128)S(1)} %get-tuple-element, ...), custom_call_target="tpu_custom_call" | custom-call | flops 20000000 | bytes 4000000 | tf_op jit(solution)/shard_map/inner_levels/pallas_call | solution.py:488
  18.9 0.0 collective-permute-done.even_in
  18.9 1.2 %collective-permute-done.1.odd_in = f32[608,128]{1,0:T(8,128)S(1)} collective-permute-done((f32[608,128]{1,0:T(8,128)S(1)}, f32[608,128]{1,0:T(8,128)S(1)}, u32[]{:S(2)}, u32[]{:S(2)}) %collective-permute-start.1) | collective-permute-done | bytes 311328 | tf_op jit(solution)/shard_map/ppermute | solution.py:775
  20.1 2.3 %small_levels.1 = (f32[42,128,128]{2,1,0:T(8,128)S(1)}, f32[16,8,128]{2,1,0:T(8,128)S(1)}) custom-call(f32[4,8,64,128]{3,2,1,0:T(8,128)S(1)} %get-tuple-element.23.v_in, f32[608,128]{1,0:T(8,128)S(1)} %get-tuple-element.24.even_own, f32[608,128]{1,0:T(8,128)S(1)} %get-tuple-element.25.odd_own, f32[608,128]{1,0:T(8,128)S(1)} %collective-permute-done.even_in, ...), custom_call_target="tpu_custom_call" | custom-call | tf_op jit(solution)/shard_map/small_levels/pallas_call | solution.py:672
  22.3 13.9 %all_to_all.5.sums_ref = f32[16,8,128]{2,1,0:T(8,128)S(1)} all-to-all(f32[16,8,128]{2,1,0:T(8,128)S(1)} %get-tuple-element.36), channel_id=1, replica_groups=mesh['grp'=8,'blk'=16] {'blk'}, dimensions={0} | all-to-all | bytes 131072 | tf_op jit(solution)/shard_map/all_to_all | solution.py:782
  36.2 3.9 %final_part.1 = f32[3,16,128,256]{3,2,1,0:T(8,128)} custom-call(f32[16,8,128]{2,1,0:T(8,128)S(1)} %all_to_all.5.sums_ref, f32[18,128,128]{2,1,0:T(8,128)S(1)} %get-tuple-element.37.inner_ref, f32[42,128,128]{2,1,0:T(8,128)S(1)} %get-tuple-element.38.wide_ref, bf16[256,256]{1,0:T(8,128)(2,1)S(1)} %get-tuple-element.39.table_ref, ...), custom_call_target="tpu_custom_call" | custom-call | tf_op jit(solution)/shard_map/final_part/pallas_call | solution.py:750
Async XLA Ops:
  0.0 13.0 %copy-start = (f32[4]{0:T(128)S(1)}, f32[4]{0:T(128)}, u32[]{:S(2)}) copy-start(f32[4]{0:T(128)} %scale_ref.5) | copy-start | bytes 52
  5.7 13.2 %collective-permute-start = (f32[608,128]{1,0:T(8,128)S(1)}, f32[608,128]{1,0:T(8,128)S(1)}, u32[]{:S(2)}, u32[]{:S(2)}) collective-permute-start(f32[608,128]{1,0:T(8,128)S(1)} %get-tuple-element.24.even_own), channel_id=1, source_target_pairs={{0,1},{1,0},{2,3},{3,2},{4,5},{5,4},{6,7},{7,6},{8,9},{9,8},{10,11... | collective-permute-start | bytes 933896 | tf_op jit(solution)/shard_map/ppermute | solution.py:776
  7.4 12.6 %collective-permute-start.1 = (f32[608,128]{1,0:T(8,128)S(1)}, f32[608,128]{1,0:T(8,128)S(1)}, u32[]{:S(2)}, u32[]{:S(2)}) collective-permute-start(f32[608,128]{1,0:T(8,128)S(1)} %get-tuple-element.25.odd_own), channel_id=1, source_target_pairs={{0,15},{1,2},{2,1},{3,4},{4,3},{5,6},{6,5},{7,8},{8,7},{9,10},{10,... | collective-permute-start | bytes 933896 | tf_op jit(solution)/shard_map/ppermute | solution.py:775

commit v4 on v3

--- a/solution.py
+++ b/solution.py
@@ -60,6 +60,9 @@
 
 
 def dot2(hi, lo, table):
+    if hi.shape[1] % 128 == 0:
+        both = jnp.concatenate([hi, lo], axis=1)
+        return jnp.dot(both, jnp.concatenate([table, table], axis=0), preferred_element_type=F32)
     return jnp.dot(hi, table, preferred_element_type=F32) + jnp.dot(
         lo, table, preferred_element_type=F32
     )
@@ -206,12 +209,12 @@
 
     for k in order[:4]:
         along_y(k)
-    along_x(0, 0)
-    along_x(7, 256 * 7)
-    side_rows(even_ref, 1 - parity, 2048)
-    side_rows(odd_ref, parity, 2560)
-    for k, ready in zip(order[4:], ((1,), (6,), (2,), (3, 4, 5))):
+    for k, ready in zip(order[4:], ((0, 7), (1,), (6,), (2, 3, 4, 5))):
         along_y(k)
+        if k == 5:
+            side_rows(odd_ref, parity, 2560)
+        if k == 3:
+            side_rows(even_ref, 1 - parity, 2048)
         for i in ready:
             along_x(i, 256 * i)
 
@@ -716,19 +719,14 @@
                 for start in range(0, NY, 16):
                     value = wide(c, e, h)[start : start + 16] * ratios[h]
                     split_at(value, hi.at[slot], lo.at[slot], NY * c + start, 128 * h)
-        for c in range(3):
-            rows = slice(NY * c, NY * c + NY)
-            fine[e, c] = dot2(hi[slot, rows], lo[slot, rows], table_ref[...])
-
-    def out_copy(step):
-        rows = pl.ds(2 * step, 2)
-        return pltpu.make_async_copy(stage.at[:, rows], out_hbm.at[:, rows], sems.at[step])
-
-    for e in range(3):
-        make_fine(e)
-    for step in range(8):
-        if step < 7:
-            make_fine(step + 3)
+        values = dot2(hi[slot], lo[slot], table_ref[...])
+        for c in range(3):
+            fine[e, c] = values[NY * c : NY * c + NY]
+
+    def out_copy(row):
+        return pltpu.make_async_copy(stage.at[:, row], out_hbm.at[:, row], sems.at[row])
+
+    def make_rows(step, both):
         for c in range(3):
             for h in range(2):
                 cols = slice(128 * h, 128 * h + 128)
@@ -736,13 +734,24 @@
                     rows = slice(start, start + 16)
                     lead = slice(LEAD + start, LEAD + start + 16)
                     centre = 3.0 * fine[step + 1, c, rows, cols]
-                    low = g0_ref[c, 2 * step, h, lead] + (centre + fine[step, c, rows, cols])
-                    high = g0_ref[c, 2 * step + 1, h, lead] + (centre + fine[step + 2, c, rows, cols])
-                    stage[c, 2 * step, rows, cols] = low
-                    stage[c, 2 * step + 1, rows, cols] = high
-        out_copy(step).start()
-    for step in range(8):
-        out_copy(step).wait()
+                    for half in both:
+                        beside = fine[step + 2 * half, c, rows, cols]
+                        stage[c, 2 * step + half, rows, cols] = g0_ref[c, 2 * step + half, h, lead] + (centre + beside)
+        for half in both:
+            out_copy(2 * step + half).start()
+
+    make_fine(0)
+    make_fine(1)
+    make_fine(2)
+    make_rows(0, (0,))
+    make_fine(3)
+    make_rows(0, (1,))
+    for step in range(1, 8):
+        if step < 7:
+            make_fine(step + 3)
+        make_rows(step, (0, 1))
+    for row in range(ROWS):
+        out_copy(row).wait()
 
 
 def final_call(sums, inner, wide, table, g0):
@@ -757,7 +766,7 @@
             pltpu.VMEM((2, 3 * NY, NZ), BF16),
             pltpu.VMEM((2, 3 * NY, NZ), BF16),
             pltpu.VMEM((10, 3, NY, NZ), F32),
-            pltpu.SemaphoreType.DMA((8,)),
+            pltpu.SemaphoreType.DMA((ROWS,)),
         ],
         compiler_params=pltpu.CompilerParams(vmem_limit_bytes=16 << 20),
         name="final_part",

time: 40.3 us -> 40.3 us (level)
  no operation moved by 1% of the time
where the time goes in v4:
time: 40.3 us; the launch traced here: 40.2 us
  Pallas kernels  17.8 us (44%)
  blocking collectives  13.9 us (34%)
  starting transfers between devices  7.25 us (18%)
  waiting for transfers between devices  1.21 us (3%)
    all_to_all x1, blocking collectives, shards(): sums = lax.all_to_all(sums, 'blk', 0, 0)  13.9 us
    pallas_call x1, Pallas kernels, linear_call(): pl.pallas_call(linear_kernel, out_shape=(jax.ShapeDtypeStruct((4, 8, 64,...  5.74 us
    ppermute x1, starting transfers between devices, shards(): odd_in = lax.ppermute(odd_own, 'blk', odd_pairs)  5.57 us
    pallas_call x1, Pallas kernels, drag_call(): pl.pallas_call(drag_kernel, out_shape=(jax.ShapeDtypeStruct((3, ROWS, 2,...  4.3 us
    pallas_call x1, Pallas kernels, final_call(): pl.pallas_call(final_kernel, out_shape=jax.ShapeDtypeStruct((3, ROWS, NY,...  3.93 us
    pallas_call x1, Pallas kernels, levels_call(): pl.pallas_call(levels_kernel, out_shape=(jax.ShapeDtypeStruct((42, NY, 12...  2.26 us
    ppermute x1, starting transfers between devices, shards(): even_in = lax.ppermute(even_own, 'blk', even_pairs)  1.68 us
    pallas_call x1, Pallas kernels, inner_call(): pl.pallas_call(inner_kernel, out_shape=(jax.ShapeDtypeStruct((3, 6, 64, 1...  1.54 us
  transfers between devices with their start and end apart: 2, of which 1 were waited for; matrix products, arithmetic and copies ran while one was open for 0% of the time, Pallas kernels for 15%

profile of v4, /device:TPU:0, one launch (start us, length us, event | category | flops | bytes accessed | tf_op | source)
XLA Modules:
  0.0 40.2 jit_solution(9269535159513227457)
XLA Ops:
  0.0 0.0 copy-start
  0.0 5.7 %linear_part.1 = (f32[4,8,64,128]{3,2,1,0:T(8,128)S(1)}, f32[608,128]{1,0:T(8,128)S(1)}, f32[608,128]{1,0:T(8,128)S(1)}, f32[4,16,2,144,128]{4,3,2,1,0:T(8,128)S(1)}, f32[2,16,32]{2,1,0:T(8,128)S(1)}) custom-call(f32[16,128,256]{2,1,0:T(8,128)} %void_hbm.1, f32[3,16,128,256]{3,2,1,0:T(8,128)} %slip_hbm.1, s32[2,16,32]{2,1,0:T(8,128)} %class_hbm.1), custom_call_target="tpu_custom_call" | custom-call | tf_op jit(solution)/shard_map/linear_part/pallas_call | solution.py:280
  5.7 1.7 %collective-permute-start = (f32[608,128]{1,0:T(8,128)S(1)}, f32[608,128]{1,0:T(8,128)S(1)}, u32[]{:S(2)}, u32[]{:S(2)}) collective-permute-start(f32[608,128]{1,0:T(8,128)S(1)} %get-tuple-element.24.even_own), channel_id=1, source_target_pairs={{0,1},{1,0},{2,3},{3,2},{4,5},{5,4},{6,7},{7,6},{8,9},{9,8},{10,11... | collective-permute-start | bytes 933896 | tf_op jit(solution)/shard_map/ppermute | solution.py:785
  7.4 5.6 %collective-permute-start.1 = (f32[608,128]{1,0:T(8,128)S(1)}, f32[608,128]{1,0:T(8,128)S(1)}, u32[]{:S(2)}, u32[]{:S(2)}) collective-permute-start(f32[608,128]{1,0:T(8,128)S(1)} %get-tuple-element.25.odd_own), channel_id=1, source_target_pairs={{0,15},{1,2},{2,1},{3,4},{4,3},{5,6},{6,5},{7,8},{8,7},{9,10},{10,... | collective-permute-start | bytes 933896 | tf_op jit(solution)/shard_map/ppermute | solution.py:784
  13.0 0.0 copy-done
  13.0 4.3 %drag_part.1 = (f32[3,16,2,144,128]{4,3,2,1,0:T(8,128)S(1)}, f32[3,8,64,128]{3,2,1,0:T(8,128)S(1)}, f32[2,3,64,128]{3,2,1,0:T(8,128)S(1)}) custom-call(f32[4,16,2,144,128]{4,3,2,1,0:T(8,128)S(1)} %get-tuple-element.26.fields, f32[2,16,32]{2,1,0:T(8,128)S(1)} %get-tuple-element.27.class_ref, f32[4]{0:T(128)S(1)} %copy-done), custom_call_target="tpu_custom_call" | custom-call | flops 60000000 | bytes 16000000 | tf_op jit(solution)/shard_map/drag_part/pallas_call | solution.py:375
  17.3 1.5 %inner_levels.1 = (f32[3,6,64,128]{3,2,1,0:T(8,128)S(1)}, f32[4,2,32,64]{3,2,1,0:T(8,128)S(1)}, f32[3,2,32,64]{3,2,1,0:T(8,128)S(1)}, f32[18,128,128]{2,1,0:T(8,...) custom-call(f32[4,8,64,128]{3,2,1,0:T(8,128)S(1)} %get-tuple-element, ...), custom_call_target="tpu_custom_call" | custom-call | flops 20000000 | bytes 4000000 | tf_op jit(solution)/shard_map/inner_levels/pallas_call | solution.py:491
  18.9 0.0 collective-permute-done.even_in
  18.9 1.2 %collective-permute-done.1.odd_in = f32[608,128]{1,0:T(8,128)S(1)} collective-permute-done((f32[608,128]{1,0:T(8,128)S(1)}, f32[608,128]{1,0:T(8,128)S(1)}, u32[]{:S(2)}, u32[]{:S(2)}) %collective-permute-start.1) | collective-permute-done | bytes 311328 | tf_op jit(solution)/shard_map/ppermute | solution.py:784
  20.1 2.3 %small_levels.1 = (f32[42,128,128]{2,1,0:T(8,128)S(1)}, f32[16,8,128]{2,1,0:T(8,128)S(1)}) custom-call(f32[4,8,64,128]{3,2,1,0:T(8,128)S(1)} %get-tuple-element.23.v_in, f32[608,128]{1,0:T(8,128)S(1)} %get-tuple-element.24.even_own, f32[608,128]{1,0:T(8,128)S(1)} %get-tuple-element.25.odd_own, f32[608,128]{1,0:T(8,128)S(1)} %collective-permute-done.even_in, ...), custom_call_target="tpu_custom_call" | custom-call | tf_op jit(solution)/shard_map/small_levels/pallas_call | solution.py:675
  22.3 13.9 %all_to_all.5.sums_ref = f32[16,8,128]{2,1,0:T(8,128)S(1)} all-to-all(f32[16,8,128]{2,1,0:T(8,128)S(1)} %get-tuple-element.36), channel_id=1, replica_groups=mesh['grp'=8,'blk'=16] {'blk'}, dimensions={0} | all-to-all | bytes 131072 | tf_op jit(solution)/shard_map/all_to_all | solution.py:791
  36.2 3.9 %final_part.1 = f32[3,16,128,256]{3,2,1,0:T(8,128)} custom-call(f32[16,8,128]{2,1,0:T(8,128)S(1)} %all_to_all.5.sums_ref, f32[18,128,128]{2,1,0:T(8,128)S(1)} %get-tuple-element.37.inner_ref, f32[42,128,128]{2,1,0:T(8,128)S(1)} %get-tuple-element.38.wide_ref, bf16[256,256]{1,0:T(8,128)(2,1)S(1)} %get-tuple-element.39.table_ref, ...), custom_call_target="tpu_custom_call" | custom-call | tf_op jit(solution)/shard_map/final_part/pallas_call | solution.py:759
Async XLA Ops:
  0.0 13.0 %copy-start = (f32[4]{0:T(128)S(1)}, f32[4]{0:T(128)}, u32[]{:S(2)}) copy-start(f32[4]{0:T(128)} %scale_ref.5) | copy-start | bytes 52
  5.7 13.1 %collective-permute-start = (f32[608,128]{1,0:T(8,128)S(1)}, f32[608,128]{1,0:T(8,128)S(1)}, u32[]{:S(2)}, u32[]{:S(2)}) collective-permute-start(f32[608,128]{1,0:T(8,128)S(1)} %get-tuple-element.24.even_own), channel_id=1, source_target_pairs={{0,1},{1,0},{2,3},{3,2},{4,5},{5,4},{6,7},{7,6},{8,9},{9,8},{10,11... | collective-permute-start | bytes 933896 | tf_op jit(solution)/shard_map/ppermute | solution.py:785
  7.4 12.7 %collective-permute-start.1 = (f32[608,128]{1,0:T(8,128)S(1)}, f32[608,128]{1,0:T(8,128)S(1)}, u32[]{:S(2)}, u32[]{:S(2)}) collective-permute-start(f32[608,128]{1,0:T(8,128)S(1)} %get-tuple-element.25.odd_own), channel_id=1, source_target_pairs={{0,15},{1,2},{2,1},{3,4},{4,3},{5,6},{6,5},{7,8},{8,7},{9,10},{10,... | collective-permute-start | bytes 933896 | tf_op jit(solution)/shard_map/ppermute | solution.py:784

commit v5 on v4

--- a/solution.py
+++ b/solution.py
@@ -209,7 +209,7 @@
 
     for k in order[:4]:
         along_y(k)
-    for k, ready in zip(order[4:], ((0, 7), (1,), (6,), (2, 3, 4, 5))):
+    for k, ready in zip(order[4:], ((0, 7), (1,), (6, 2), (3, 4, 5))):
         along_y(k)
         if k == 5:
             side_rows(odd_ref, parity, 2560)
@@ -647,7 +647,7 @@
     sums += [total(numerator), total(denominator)]
     ones = jnp.ones((1, 32), F32)
     packed = [sums[0], sums[1]] + [jnp.concatenate([sums[2 + k], sums[4 + k], ones], axis=1) for k in range(2)]
-    tile = jnp.concatenate(packed + [jnp.zeros((4, 128), F32)], axis=0)
+    tile = jnp.concatenate(packed, axis=0)
     for d in range(16):
         sums_ref[d] = tile
 
@@ -676,7 +676,7 @@
         levels_kernel,
         out_shape=(
             jax.ShapeDtypeStruct((42, NY, 128), F32),
-            jax.ShapeDtypeStruct((16, 8, 128), F32),
+            jax.ShapeDtypeStruct((16, 4, 128), F32),
         ),
         in_specs=[vmem] * 8 + [pl.BlockSpec(memory_space=pltpu.SMEM)] + [vmem] * 6,
         out_specs=(vmem,) * 2,

time: 40.3 us -> 40.2 us (level)
  no operation moved by 1% of the time
where the time goes in v5:
time: 40.2 us; the launch traced here: 40.1 us
  Pallas kernels  17.7 us (44%)
  blocking collectives  13.8 us (34%)
  starting transfers between devices  7.25 us (18%)
  waiting for transfers between devices  1.21 us (3%)
    all_to_all x1, blocking collectives, shards(): sums = lax.all_to_all(sums, 'blk', 0, 0)  13.8 us
    pallas_call x1, Pallas kernels, linear_call(): pl.pallas_call(linear_kernel, out_shape=(jax.ShapeDtypeStruct((4, 8, 64,...  5.69 us
    ppermute x1, starting transfers between devices, shards(): odd_in = lax.ppermute(odd_own, 'blk', odd_pairs)  5.57 us
    pallas_call x1, Pallas kernels, drag_call(): pl.pallas_call(drag_kernel, out_shape=(jax.ShapeDtypeStruct((3, ROWS, 2,...  4.3 us
    pallas_call x1, Pallas kernels, final_call(): pl.pallas_call(final_kernel, out_shape=jax.ShapeDtypeStruct((3, ROWS, NY,...  3.92 us
    pallas_call x1, Pallas kernels, levels_call(): pl.pallas_call(levels_kernel, out_shape=(jax.ShapeDtypeStruct((42, NY, 12...  2.26 us
    ppermute x1, starting transfers between devices, shards(): even_in = lax.ppermute(even_own, 'blk', even_pairs)  1.68 us
    pallas_call x1, Pallas kernels, inner_call(): pl.pallas_call(inner_kernel, out_shape=(jax.ShapeDtypeStruct((3, 6, 64, 1...  1.53 us
  transfers between devices with their start and end apart: 2, of which 1 were waited for; matrix products, arithmetic and copies ran while one was open for 0% of the time, Pallas kernels for 15%

profile of v5, /device:TPU:0, one launch (start us, length us, event | category | flops | bytes accessed | tf_op | source)
XLA Modules:
  0.0 40.1 jit_solution(9120854910085812802)
XLA Ops:
  0.0 0.0 copy-start
  0.0 5.7 %linear_part.1 = (f32[4,8,64,128]{3,2,1,0:T(8,128)S(1)}, f32[608,128]{1,0:T(8,128)S(1)}, f32[608,128]{1,0:T(8,128)S(1)}, f32[4,16,2,144,128]{4,3,2,1,0:T(8,128)S(1)}, f32[2,16,32]{2,1,0:T(8,128)S(1)}) custom-call(f32[16,128,256]{2,1,0:T(8,128)} %void_hbm.1, f32[3,16,128,256]{3,2,1,0:T(8,128)} %slip_hbm.1, s32[2,16,32]{2,1,0:T(8,128)} %class_hbm.1), custom_call_target="tpu_custom_call" | custom-call | tf_op jit(solution)/shard_map/linear_part/pallas_call | solution.py:280
  5.7 1.7 %collective-permute-start = (f32[608,128]{1,0:T(8,128)S(1)}, f32[608,128]{1,0:T(8,128)S(1)}, u32[]{:S(2)}, u32[]{:S(2)}) collective-permute-start(f32[608,128]{1,0:T(8,128)S(1)} %get-tuple-element.24.even_own), channel_id=1, source_target_pairs={{0,1},{1,0},{2,3},{3,2},{4,5},{5,4},{6,7},{7,6},{8,9},{9,8},{10,11... | collective-permute-start | bytes 933896 | tf_op jit(solution)/shard_map/ppermute | solution.py:785
  7.4 5.6 %collective-permute-start.1 = (f32[608,128]{1,0:T(8,128)S(1)}, f32[608,128]{1,0:T(8,128)S(1)}, u32[]{:S(2)}, u32[]{:S(2)}) collective-permute-start(f32[608,128]{1,0:T(8,128)S(1)} %get-tuple-element.25.odd_own), channel_id=1, source_target_pairs={{0,15},{1,2},{2,1},{3,4},{4,3},{5,6},{6,5},{7,8},{8,7},{9,10},{10,... | collective-permute-start | bytes 933896 | tf_op jit(solution)/shard_map/ppermute | solution.py:784
  13.0 0.0 copy-done
  13.0 4.3 %drag_part.1 = (f32[3,16,2,144,128]{4,3,2,1,0:T(8,128)S(1)}, f32[3,8,64,128]{3,2,1,0:T(8,128)S(1)}, f32[2,3,64,128]{3,2,1,0:T(8,128)S(1)}) custom-call(f32[4,16,2,144,128]{4,3,2,1,0:T(8,128)S(1)} %get-tuple-element.26.fields, f32[2,16,32]{2,1,0:T(8,128)S(1)} %get-tuple-element.27.class_ref, f32[4]{0:T(128)S(1)} %copy-done), custom_call_target="tpu_custom_call" | custom-call | flops 60000000 | bytes 16000000 | tf_op jit(solution)/shard_map/drag_part/pallas_call | solution.py:375
  17.3 1.5 %inner_levels.1 = (f32[3,6,64,128]{3,2,1,0:T(8,128)S(1)}, f32[4,2,32,64]{3,2,1,0:T(8,128)S(1)}, f32[3,2,32,64]{3,2,1,0:T(8,128)S(1)}, f32[18,128,128]{2,1,0:T(8,...) custom-call(f32[4,8,64,128]{3,2,1,0:T(8,128)S(1)} %get-tuple-element, ...), custom_call_target="tpu_custom_call" | custom-call | flops 20000000 | bytes 4000000 | tf_op jit(solution)/shard_map/inner_levels/pallas_call | solution.py:491
  18.8 0.0 collective-permute-done.even_in
  18.8 1.2 %collective-permute-done.1.odd_in = f32[608,128]{1,0:T(8,128)S(1)} collective-permute-done((f32[608,128]{1,0:T(8,128)S(1)}, f32[608,128]{1,0:T(8,128)S(1)}, u32[]{:S(2)}, u32[]{:S(2)}) %collective-permute-start.1) | collective-permute-done | bytes 311328 | tf_op jit(solution)/shard_map/ppermute | solution.py:784
  20.0 2.3 %small_levels.1 = (f32[42,128,128]{2,1,0:T(8,128)S(1)}, f32[16,4,128]{2,1,0:T(4,128)S(1)}) custom-call(f32[4,8,64,128]{3,2,1,0:T(8,128)S(1)} %get-tuple-element.23.v_in, f32[608,128]{1,0:T(8,128)S(1)} %get-tuple-element.24.even_own, f32[608,128]{1,0:T(8,128)S(1)} %get-tuple-element.25.odd_own, f32[608,128]{1,0:T(8,128)S(1)} %collective-permute-done.even_in, ...), custom_call_target="tpu_custom_call" | custom-call | tf_op jit(solution)/shard_map/small_levels/pallas_call | solution.py:675
  22.3 13.8 %all_to_all.5.sums_ref = f32[16,4,128]{2,1,0:T(4,128)S(1)} all-to-all(f32[16,4,128]{2,1,0:T(4,128)S(1)} %get-tuple-element.36), channel_id=1, replica_groups=mesh['grp'=8,'blk'=16] {'blk'}, dimensions={0} | all-to-all | bytes 65536 | tf_op jit(solution)/shard_map/all_to_all | solution.py:791
  36.1 3.9 %final_part.1 = f32[3,16,128,256]{3,2,1,0:T(8,128)} custom-call(f32[16,4,128]{2,1,0:T(4,128)S(1)} %all_to_all.5.sums_ref, f32[18,128,128]{2,1,0:T(8,128)S(1)} %get-tuple-element.37.inner_ref, f32[42,128,128]{2,1,0:T(8,128)S(1)} %get-tuple-element.38.wide_ref, bf16[256,256]{1,0:T(8,128)(2,1)S(1)} %get-tuple-element.39.table_ref, ...), custom_call_target="tpu_custom_call" | custom-call | tf_op jit(solution)/shard_map/final_part/pallas_call | solution.py:759
Async XLA Ops:
  0.0 13.0 %copy-start = (f32[4]{0:T(128)S(1)}, f32[4]{0:T(128)}, u32[]{:S(2)}) copy-start(f32[4]{0:T(128)} %scale_ref.5) | copy-start | bytes 52
  5.7 13.1 %collective-permute-start = (f32[608,128]{1,0:T(8,128)S(1)}, f32[608,128]{1,0:T(8,128)S(1)}, u32[]{:S(2)}, u32[]{:S(2)}) collective-permute-start(f32[608,128]{1,0:T(8,128)S(1)} %get-tuple-element.24.even_own), channel_id=1, source_target_pairs={{0,1},{1,0},{2,3},{3,2},{4,5},{5,4},{6,7},{7,6},{8,9},{9,8},{10,11... | collective-permute-start | bytes 933896 | tf_op jit(solution)/shard_map/ppermute | solution.py:785
  7.4 12.6 %collective-permute-start.1 = (f32[608,128]{1,0:T(8,128)S(1)}, f32[608,128]{1,0:T(8,128)S(1)}, u32[]{:S(2)}, u32[]{:S(2)}) collective-permute-start(f32[608,128]{1,0:T(8,128)S(1)} %get-tuple-element.25.odd_own), channel_id=1, source_target_pairs={{0,15},{1,2},{2,1},{3,4},{4,3},{5,6},{6,5},{7,8},{8,7},{9,10},{10,... | collective-permute-start | bytes 933896 | tf_op jit(solution)/shard_map/ppermute | solution.py:784
